TPU v7x, 32 devices: a whole 2x2x4 slice. The times are simulated.
32 devices in a mesh: head: 4 (over x, core), blk: 8 (over z, y).
Axes of the slice: x: 2, y: 2, z: 4, core: 2. Of those that a mesh axis runs over, the one named last changes fastest.
Arguments:
- inputs: bfloat16 [4096, 512], P(('blk', 'head')), may hold values from -6 to 6
- ln1_gain: bfloat16 [512], P('blk'), may hold values from 0.5 to 1.5
- w_qkv: bfloat16 [512, 1536], P('blk'), may hold values from -0.25 to 0.25
- w_out: bfloat16 [512, 512], P('blk'), may hold values from -2 to 2
- ln2_gain: bfloat16 [512], P('blk'), may hold values from 0.5 to 1.5
- w_router: bfloat16 [512, 8], P('blk'), may hold values from -0.25 to 0.25
- expert_in: bfloat16 [8, 512, 2048], P('blk'), may hold values from -0.25 to 0.25
- expert_out: bfloat16 [8, 2048, 512], P('blk'), may hold values from -2 to 2
- routes: int32 [4096, 2], P(('blk', 'head')), may hold values from 0 to 7, all different within a row
- priority: int32 [32, 128], P(('blk', 'head')), may hold values from 0 to 127, each once within a row
- doc_lengths: int32 [16], replicated, may hold values from 1 to 2048, 4096 in all
- d_out: float32 [4096, 512], P(('blk', 'head')), may hold values from -6 to 6
Outputs:
- output: bfloat16 [4096, 512], P(('blk', 'head'))
- d_inputs: float32 [4096, 512], P(('blk', 'head'))
- d_ln1_gain: float32 [512], P('blk')
- d_w_qkv: float32 [512, 1536], P('blk')
- d_w_out: float32 [512, 512], P('blk')
- d_ln2_gain: float32 [512], P('blk')
- d_w_router: float32 [512, 8], P('blk')
- d_expert_in: float32 [8, 512, 2048], P('blk')
- d_expert_out: float32 [8, 2048, 512], P('blk')
Inputs may be any that keep to these rules, and one draw needn't show every extreme that they name: `routes`: each token names two different experts. `priority`: each row holds every rank from 0 to 127 once. `doc_lengths`: the documents' lengths sum to 4096; the longest has exactly 2048 tokens.
All inputs are finite; a program needn't handle non-finite values.
Results may differ from a plain program's by a relative error of at most 0.022.
Values may be sent and summed in bfloat16 or wider, within the bound.
A program may use at most 128 MiB of HBM per device.

v0:
```python
import functools
import math

import jax
import jax.numpy as jnp
from jax import lax
from jax.experimental import pallas as pl
from jax.experimental.pallas import tpu as pltpu
from jax.sharding import PartitionSpec as P

HS = 64
KEY_BLOCK = 2048


PRECISE = lax.Precision.HIGHEST
MASKED = -1e30
EPSILON = 1e-06


def layer_norm(values, gain):
    average = jnp.mean(values, axis=-1, keepdims=True)
    centred = values - average
    spread = jnp.mean(centred * centred, axis=-1, keepdims=True)
    return centred * lax.rsqrt(spread + EPSILON) * gain


def gelu_exact(values):
    return jax.nn.gelu(values, approximate=False)


def router(row_block, weight):
    return jax.nn.softmax(jnp.dot(row_block, weight, precision=PRECISE), axis=-1)


def doc_index(positions, doc_lengths):
    places = jnp.arange(doc_lengths.shape[0], dtype=jnp.int32)
    starts = jnp.sum(jnp.where(places[None, :] < places[:, None], doc_lengths[None, :], 0), axis=1)
    at_most = (starts[None, :] <= positions[:, None]).astype(jnp.int32)
    return jnp.sum(at_most, axis=1) - 1


def slot_table(route_rows, ranking, capacity):
    token_count = route_rows.shape[0]
    expert = jnp.transpose(route_rows).reshape(-1)
    pair_order = (jnp.arange(2, dtype=jnp.int32)[:, None] * token_count + ranking[None, :]).reshape(
        -1
    )
    before = (expert[:, None] == expert[None, :]) & (pair_order[None, :] < pair_order[:, None])
    position = jnp.sum(before.astype(jnp.int32), axis=1)
    slot_ids = jnp.where(position < capacity, expert * capacity + position, -1)
    return slot_ids.reshape(2, token_count)


def keep_state(current):
    return current


def local(
    inputs,
    ln1_gain,
    w_qkv,
    w_out,
    ln2_gain,
    w_router,
    expert_in,
    expert_out,
    routes,
    priority,
    doc_lengths,
    d_out,
):
    blk_size = lax.axis_size("blk")
    tok_rows = inputs.shape[0]
    model_width = inputs.shape[1]
    capacity = 2 * tok_rows // blk_size
    slot_total = blk_size * capacity
    gain_one, qkv_weight, out_weight, gain_two, router_weight = (
        lax.all_gather(ln1_gain, "blk", axis=0, tiled=True),
        lax.all_gather(w_qkv, "blk", axis=0, tiled=True),
        lax.all_gather(w_out, "blk", axis=0, tiled=True),
        lax.all_gather(ln2_gain, "blk", axis=0, tiled=True),
        lax.all_gather(w_router, "blk", axis=0, tiled=True),
    )
    input_rows = inputs.astype(jnp.float32)
    normed_one, norm_one_pull = jax.vjp(layer_norm, input_rows, gain_one.astype(jnp.float32))
    normed_low = normed_one.astype(jnp.bfloat16)
    qkv_rows = jnp.dot(normed_low, qkv_weight, preferred_element_type=jnp.float32).astype(
        jnp.bfloat16
    )
    query_heads, key_heads, value_heads = (
        lax.all_to_all(qkv_rows[:, :model_width], "head", split_axis=1, concat_axis=0, tiled=True),
        lax.all_to_all(
            qkv_rows[:, model_width : 2 * model_width],
            "head",
            split_axis=1,
            concat_axis=0,
            tiled=True,
        ),
        lax.all_to_all(
            qkv_rows[:, 2 * model_width :], "head", split_axis=1, concat_axis=0, tiled=True
        ),
    )
    span_rows = query_heads.shape[0]
    head_count = query_heads.shape[1] // HS
    key_all, value_all = (
        lax.all_gather(key_heads, "blk", axis=0, tiled=True),
        lax.all_gather(value_heads, "blk", axis=0, tiled=True),
    )
    total_rows = key_all.shape[0]
    block_count = total_rows // KEY_BLOCK
    scale_factor = HS ** (-0.5)
    query_pos = lax.axis_index("blk") * span_rows + jnp.arange(span_rows, dtype=jnp.int32)
    query_docs = doc_index(query_pos, doc_lengths)
    queries = query_heads.reshape(span_rows, head_count, HS)

    def block_parts(block_index, key_source, value_source):
        first_key = block_index * KEY_BLOCK
        key_rows = lax.dynamic_slice_in_dim(key_source, first_key, KEY_BLOCK, 0).reshape(
            KEY_BLOCK, head_count, HS
        )
        value_rows = lax.dynamic_slice_in_dim(value_source, first_key, KEY_BLOCK, 0).reshape(
            KEY_BLOCK, head_count, HS
        )
        key_docs = doc_index(first_key + jnp.arange(KEY_BLOCK, dtype=jnp.int32), doc_lengths)
        is_live = (key_docs[0] <= query_docs[-1]) & (key_docs[-1] >= query_docs[0])
        same_doc = query_docs[:, None] == key_docs[None, :]
        return (first_key, key_rows, value_rows, same_doc, is_live)

    def block_scores(key_rows, same_doc):
        raw_scores = (
            jnp.einsum("qhd,khd->hqk", queries, key_rows, preferred_element_type=jnp.float32)
            * scale_factor
        )
        return jnp.where(same_doc[None], raw_scores, MASKED)

    def stat_step(block_index, loop_state):
        first_key, key_rows, value_rows, same_doc, is_live = block_parts(
            block_index, key_all, value_all
        )

        def stat_update(current):
            running_max, running_sum = current
            scores = block_scores(key_rows, same_doc)
            new_max = jnp.maximum(running_max, jnp.max(scores, axis=2))
            exp_terms = jnp.where(same_doc[None], jnp.exp(scores - new_max[:, :, None]), 0.0)
            return (
                new_max,
                running_sum * jnp.exp(running_max - new_max) + jnp.sum(exp_terms, axis=2),
            )

        return lax.cond(is_live, stat_update, keep_state, loop_state)

    start_state = (
        jnp.full((head_count, span_rows), MASKED, jnp.float32),
        jnp.zeros((head_count, span_rows), jnp.float32),
    )
    running_max, running_sum = lax.fori_loop(0, block_count, stat_step, start_state)
    log_total = running_max + jnp.log(running_sum)

    def out_step(block_index, loop_state):
        first_key, key_rows, value_rows, same_doc, is_live = block_parts(
            block_index, key_all, value_all
        )

        def out_update(current):
            scores = block_scores(key_rows, same_doc)
            weights = jnp.where(
                same_doc[None], jnp.exp(scores - log_total[:, :, None]), 0.0
            ).astype(jnp.bfloat16)
            return current + jnp.einsum(
                "hqk,khd->qhd", weights, value_rows, preferred_element_type=jnp.float32
            )

        return lax.cond(is_live, out_update, keep_state, loop_state)

    mixed_full = lax.fori_loop(
        0, block_count, out_step, jnp.zeros((span_rows, head_count, HS), jnp.float32)
    )
    mixed_low = mixed_full.reshape(span_rows, head_count * HS).astype(jnp.bfloat16)
    mixed_tokens = lax.all_to_all(mixed_low, "head", split_axis=0, concat_axis=1, tiled=True)
    attended = jnp.dot(mixed_tokens, out_weight, preferred_element_type=jnp.float32)
    hidden_one = input_rows + attended
    normed_two, norm_two_pull = jax.vjp(layer_norm, hidden_one, gain_two.astype(jnp.float32))
    routed_low = normed_two.astype(jnp.bfloat16)
    router_probs, router_pull = jax.vjp(
        router, routed_low.astype(jnp.float32), router_weight.astype(jnp.float32)
    )
    slot_ids = slot_table(routes, priority[0], capacity)
    select = (
        slot_ids[:, :, None] == jnp.arange(slot_total, dtype=jnp.int32)[None, None, :]
    ).astype(jnp.bfloat16)
    send_rows = jnp.einsum(
        "kts,td->sd", select, routed_low, preferred_element_type=jnp.float32
    ).astype(jnp.bfloat16)
    expert_rows = lax.all_to_all(
        send_rows.reshape(blk_size, capacity, model_width),
        "blk",
        split_axis=0,
        concat_axis=0,
        tiled=True,
    ).reshape(slot_total, model_width)
    weight_in = expert_in[0]
    weight_out = expert_out[0]
    pre_act = jnp.dot(expert_rows, weight_in, preferred_element_type=jnp.float32)
    hidden_act, gelu_pull = jax.vjp(gelu_exact, pre_act)
    hidden_low = hidden_act.astype(jnp.bfloat16)
    expert_result = jnp.dot(hidden_low, weight_out, preferred_element_type=jnp.float32).astype(
        jnp.bfloat16
    )
    slot_result = lax.all_to_all(
        expert_result.reshape(blk_size, capacity, model_width),
        "blk",
        split_axis=0,
        concat_axis=0,
        tiled=True,
    ).reshape(slot_total, model_width)
    pair_result = jnp.einsum("kts,sd->ktd", select, slot_result, preferred_element_type=jnp.float32)
    route_hot = (routes[:, :, None] == jnp.arange(blk_size, dtype=jnp.int32)[None, None, :]).astype(
        jnp.float32
    )
    gate_vals = jnp.sum(router_probs[:, None, :] * route_hot, axis=2)
    mixture = gate_vals[:, 0, None] * pair_result[0] + gate_vals[:, 1, None] * pair_result[1]
    output = (hidden_one + mixture).astype(jnp.bfloat16)
    d_gates = jnp.transpose(jnp.sum(d_out[None] * pair_result, axis=2))
    d_probs = jnp.sum(d_gates[:, :, None] * route_hot, axis=1)
    pair_grads = (jnp.transpose(gate_vals)[:, :, None] * d_out[None]).astype(jnp.bfloat16)
    slot_grads = jnp.einsum(
        "kts,ktd->sd", select, pair_grads, preferred_element_type=jnp.float32
    ).astype(jnp.bfloat16)
    result_grads = lax.all_to_all(
        slot_grads.reshape(blk_size, capacity, model_width),
        "blk",
        split_axis=0,
        concat_axis=0,
        tiled=True,
    ).reshape(slot_total, model_width)
    d_hidden_act = jnp.dot(result_grads, weight_out.T, preferred_element_type=jnp.float32)
    d_weight_out = jnp.dot(hidden_low.T, result_grads, preferred_element_type=jnp.float32)
    d_preact = gelu_pull(d_hidden_act)[0].astype(jnp.bfloat16)
    d_weight_in = jnp.dot(expert_rows.T, d_preact, preferred_element_type=jnp.float32)
    row_grads = jnp.dot(d_preact, weight_in.T, preferred_element_type=jnp.float32).astype(
        jnp.bfloat16
    )
    slot_back = lax.all_to_all(
        row_grads.reshape(blk_size, capacity, model_width),
        "blk",
        split_axis=0,
        concat_axis=0,
        tiled=True,
    ).reshape(slot_total, model_width)
    d_routed = jnp.einsum("kts,sd->td", select, slot_back, preferred_element_type=jnp.float32)
    d_routed_router, d_router = router_pull(d_probs)
    d_hidden_norm, d_gain_two = norm_two_pull(d_routed + d_routed_router)
    d_hidden_one = d_out + d_hidden_norm
    attn_grads = d_hidden_one.astype(jnp.bfloat16)
    d_out_weight = jnp.dot(mixed_tokens.T, attn_grads, preferred_element_type=jnp.float32)
    mixed_grads = jnp.dot(attn_grads, out_weight.T, preferred_element_type=jnp.float32).astype(
        jnp.bfloat16
    )
    head_grads = lax.all_to_all(mixed_grads, "head", split_axis=1, concat_axis=0, tiled=True)
    out_grads = head_grads.reshape(span_rows, head_count, HS)
    row_delta = jnp.transpose(jnp.sum(out_grads.astype(jnp.float32) * mixed_full, axis=2))
    key_back, value_back = (
        lax.all_gather(key_heads, "blk", axis=0, tiled=True),
        lax.all_gather(value_heads, "blk", axis=0, tiled=True),
    )

    def grad_step(block_index, loop_state):
        first_key, key_rows, value_rows, same_doc, is_live = block_parts(
            block_index, key_back, value_back
        )

        def grad_update(current):
            query_grad, key_grad, value_grad = current
            scores = block_scores(key_rows, same_doc)
            weights = jnp.where(same_doc[None], jnp.exp(scores - log_total[:, :, None]), 0.0)
            value_part = jnp.einsum(
                "hqk,qhd->khd",
                weights.astype(jnp.bfloat16),
                out_grads,
                preferred_element_type=jnp.float32,
            )
            weight_grads = jnp.einsum(
                "qhd,khd->hqk", out_grads, value_rows, preferred_element_type=jnp.float32
            )
            score_grads = (weights * (weight_grads - row_delta[:, :, None])).astype(jnp.bfloat16)
            query_grad = (
                query_grad
                + jnp.einsum(
                    "hqk,khd->qhd", score_grads, key_rows, preferred_element_type=jnp.float32
                )
                * scale_factor
            )
            key_part = (
                jnp.einsum("hqk,qhd->khd", score_grads, queries, preferred_element_type=jnp.float32)
                * scale_factor
            )
            key_grad = lax.dynamic_update_slice_in_dim(
                key_grad, key_part.reshape(KEY_BLOCK, head_count * HS), first_key, 0
            )
            value_grad = lax.dynamic_update_slice_in_dim(
                value_grad, value_part.reshape(KEY_BLOCK, head_count * HS), first_key, 0
            )
            return (query_grad, key_grad, value_grad)

        return lax.cond(is_live, grad_update, keep_state, loop_state)

    start_grads = (
        jnp.zeros((span_rows, head_count, HS), jnp.float32),
        jnp.zeros((total_rows, head_count * HS), jnp.float32),
        jnp.zeros((total_rows, head_count * HS), jnp.float32),
    )
    query_grad, key_grad, value_grad = lax.fori_loop(0, block_count, grad_step, start_grads)
    key_own, value_own = (
        lax.psum_scatter(
            key_grad.astype(jnp.bfloat16), "blk", scatter_dimension=0, tiled=True
        ).astype(jnp.float32),
        lax.psum_scatter(
            value_grad.astype(jnp.bfloat16), "blk", scatter_dimension=0, tiled=True
        ).astype(jnp.float32),
    )
    query_tokens_grad, key_tokens_grad, value_tokens_grad = (
        lax.all_to_all(
            query_grad.reshape(span_rows, head_count * HS).astype(jnp.bfloat16),
            "head",
            split_axis=0,
            concat_axis=1,
            tiled=True,
        ),
        lax.all_to_all(
            key_own.astype(jnp.bfloat16), "head", split_axis=0, concat_axis=1, tiled=True
        ),
        lax.all_to_all(
            value_own.astype(jnp.bfloat16), "head", split_axis=0, concat_axis=1, tiled=True
        ),
    )
    qkv_grads = jnp.concatenate([query_tokens_grad, key_tokens_grad, value_tokens_grad], axis=1)
    d_qkv_weight = jnp.dot(normed_low.T, qkv_grads, preferred_element_type=jnp.float32)
    normed_grads = jnp.dot(qkv_grads, qkv_weight.T, preferred_element_type=jnp.float32)
    d_inputs_norm, d_gain_one = norm_one_pull(normed_grads)
    d_inputs = d_hidden_one + d_inputs_norm
    gain_one_sum, qkv_sum, out_sum, gain_two_sum, router_sum = (
        lax.psum_scatter(
            d_gain_one.astype(jnp.bfloat16), "blk", scatter_dimension=0, tiled=True
        ).astype(jnp.float32),
        lax.psum_scatter(
            d_qkv_weight.astype(jnp.bfloat16), "blk", scatter_dimension=0, tiled=True
        ).astype(jnp.float32),
        lax.psum_scatter(
            d_out_weight.astype(jnp.bfloat16), "blk", scatter_dimension=0, tiled=True
        ).astype(jnp.float32),
        lax.psum_scatter(
            d_gain_two.astype(jnp.bfloat16), "blk", scatter_dimension=0, tiled=True
        ).astype(jnp.float32),
        lax.psum_scatter(
            d_router.astype(jnp.bfloat16), "blk", scatter_dimension=0, tiled=True
        ).astype(jnp.float32),
    )
    gain_one_all, qkv_all, out_all, gain_two_all, router_all, expert_in_all, expert_out_all = (
        lax.psum(gain_one_sum.astype(jnp.bfloat16), "head").astype(jnp.float32),
        lax.psum(qkv_sum.astype(jnp.bfloat16), "head").astype(jnp.float32),
        lax.psum(out_sum.astype(jnp.bfloat16), "head").astype(jnp.float32),
        lax.psum(gain_two_sum.astype(jnp.bfloat16), "head").astype(jnp.float32),
        lax.psum(router_sum.astype(jnp.bfloat16), "head").astype(jnp.float32),
        lax.psum(d_weight_in[None].astype(jnp.bfloat16), "head").astype(jnp.float32),
        lax.psum(d_weight_out[None].astype(jnp.bfloat16), "head").astype(jnp.float32),
    )
    return (
        output,
        d_inputs,
        gain_one_all,
        qkv_all,
        out_all,
        gain_two_all,
        router_all,
        expert_in_all,
        expert_out_all,
    )


MESH = pl.DeviceIdType.MESH
LANES = 128
HALF = LANES // 2
MIB = 2**20
F32 = jnp.float32
BF16 = jnp.bfloat16


def dot(left, right, dims=(1, 0)):
    return lax.dot_general(
        left, right, (((dims[0],), (dims[1],)), ((), ())), preferred_element_type=F32
    )


def remote(src, dst, send_sem, recv_sem, head, blk):
    return pltpu.make_async_remote_copy(
        src_ref=src,
        dst_ref=dst,
        send_sem=send_sem,
        recv_sem=recv_sem,
        device_id={"head": head, "blk": blk},
        device_id_type=MESH,
    )


def arrived(ref, sem):
    pltpu.make_async_copy(ref, ref, sem).wait()


def greet(peers):
    barrier = pltpu.get_barrier_semaphore()
    for head, blk in peers:
        pl.semaphore_signal(
            barrier, inc=1, device_id={"head": head, "blk": blk}, device_id_type=MESH
        )
    return len(peers)


def meet(count):
    pl.semaphore_wait(pltpu.get_barrier_semaphore(), count)


def halves(values, lanes_kept):
    rows = values.shape[0] // 2
    moved = pltpu.roll(values[rows:], HALF, 1)
    return jnp.where(lanes_kept, values[:rows], moved)


def lane_ids(shape):
    return lax.broadcasted_iota(jnp.int32, shape, len(shape) - 1)


def centre(values):
    average = jnp.mean(values, axis=-1, keepdims=True)
    centred = values - average
    spread = jnp.mean(centred * centred, axis=-1, keepdims=True)
    scale = lax.rsqrt(spread + EPSILON)
    return centred * scale, scale


def centre_back(grad, xhat, scale):
    middle = jnp.mean(grad, axis=-1, keepdims=True)
    along = jnp.mean(grad * xhat, axis=-1, keepdims=True)
    return (grad - middle - xhat * along) * scale


def split_high_low(column, lanes):
    high = column.astype(BF16)
    low = (column - high.astype(F32)).astype(BF16)
    return jnp.where(lanes < HALF, high.astype(F32), low.astype(F32)).astype(BF16)


def join_high_low(matrix, start):
    return matrix[:, start : start + 1].astype(F32) + matrix[
        :, start + HALF : start + HALF + 1
    ].astype(F32)


def place():
    head, blk = lax.axis_index("head"), lax.axis_index("blk")
    return head, blk, blk // 2, lax.rem(blk, 2)


def around(index, step, size):
    return lax.rem(index + step, size)


QUERY_TILE = 256
CHAINS = 2


def masked_queries(q_ref, tile, key_lanes, query_tile):
    tiles_per_span = q_ref.shape[1] // query_tile
    inner = tile % tiles_per_span * query_tile
    query = q_ref[tile // tiles_per_span, inner : inner + query_tile, :]
    return jnp.where(key_lanes, query, jnp.zeros_like(query))


def group_blocks(bounds_ref, group, size, key_tile):
    first, last = group * size, (group + 1) * size
    low = jnp.min(bounds_ref[0:1, first : first + LANES])
    high = jnp.max(bounds_ref[1:2, last - LANES : last])
    return low // key_tile, (high + key_tile - 1) // key_tile


def inside_document(bounds_ref, tile, first, shape):
    key = first + lax.broadcasted_iota(jnp.int32, shape, 0)
    columns = slice(tile * shape[1], (tile + 1) * shape[1])
    return jnp.logical_and(key >= bounds_ref[0:1, columns], key < bounds_ref[1:2, columns])


def query_group(q_ref, group, y):
    key_lanes = (lane_ids((QUERY_TILE, LANES)) < HALF) == (y == 0)
    tiles = range(group * CHAINS, (group + 1) * CHAINS)
    return tiles, [masked_queries(q_ref, tile, key_lanes, QUERY_TILE) for tile in tiles]


def attend(bounds_ref, tiles, first, keys, keys_across, queries, carry):
    scores = [dot(keys, query, (1, 1)) for query in queries]
    made = []
    for tile, score, (biggest, weight, mixed) in zip(tiles, scores, carry):
        inside = inside_document(bounds_ref, tile, first, score.shape)
        score = jnp.where(inside, score, MASKED)
        bigger = jnp.maximum(biggest, jnp.max(score, axis=0, keepdims=True))
        fade = jnp.exp(biggest - bigger)
        terms = jnp.exp(score - bigger)
        weight = weight * fade + jnp.sum(terms, axis=0, keepdims=True)
        made.append((bigger, weight, mixed * fade + dot(keys_across, terms.astype(BF16))))
    return tuple(made)


def nothing_attended():
    return (
        jnp.full((1, QUERY_TILE), MASKED, F32),
        jnp.zeros((1, QUERY_TILE), F32),
        jnp.zeros((LANES, QUERY_TILE), F32),
    )


def attend_back(bounds_ref, tiles, first, keys, keys_across, group, carry):
    queries, out_grads, deltas, log_totals = group
    scores = [dot(keys, query, (1, 1)) for query in queries]
    weight_grads = [dot(keys, out_grad, (1, 1)) for out_grad in out_grads]
    pieces, score_grads = [], []
    for i, tile in enumerate(tiles):
        inside = inside_document(bounds_ref, tile, first, scores[i].shape)
        weights = jnp.exp(jnp.where(inside, scores[i], MASKED) - log_totals[i])
        score_grads.append((weights * (weight_grads[i] - deltas[i])).astype(BF16))
        pieces.append(weights.astype(BF16))
    wide = jnp.concatenate(score_grads + pieces, axis=1)
    given = dot(wide, jnp.concatenate(queries + out_grads, axis=0))
    return given, tuple(c + dot(keys_across, g) for c, g in zip(carry, score_grads))


def group_grads(do_ref, tiles, y):
    key_lanes = (lane_ids((QUERY_TILE, LANES)) < HALF) == (y == 0)
    out_grads = []
    for tile in tiles:
        parts = []
        for part in range(QUERY_TILE // LANES):
            packed = do_ref[tile, part].astype(F32)
            parts += [packed, pltpu.roll(packed, HALF, 1)]
        out_grads.append(jnp.where(key_lanes, 0.0, jnp.concatenate(parts, axis=0)).astype(BF16))
    return out_grads


def qkv_kernel(
    heads, blks,
    x_hbm, w_hbm, g1_hbm, wo_hbm, wr_hbm, g2_hbm, docs_hbm,
    qall, kvall, xall, wall, wo_all, kvt, bounds, begun,
    x_ref, w_ref, rows_in, g1_ref, g2_ref, wr_ref, docs_ref, wo_own, kv_other, q_packed, q_landed, in_sem,
    x_send, x_recv, w_send, w_recv, o_send, o_recv, p_send, p_recv,
    k_send, k_recv, q_recv,
):
    head, blk, z, y = place()
    planes = blks // 2
    model = x_ref.shape[1]
    rows = w_ref.shape[0]
    part = rows // heads
    experts = wr_ref.shape[0]
    wanted = (
        (w_hbm, w_ref), (g1_hbm, g1_ref), (g2_hbm, g2_ref), (wr_hbm, wr_ref), (x_hbm, x_ref),
        (wo_hbm, wo_own.at[:, pl.ds(0, model)]), (docs_hbm, docs_ref),
    )
    fetched = [
        pltpu.make_async_copy(src, dst, in_sem.at[i]) for i, (src, dst) in enumerate(wanted)
    ]
    for copy in fetched:
        copy.start()
    rows_in[...] = jnp.zeros_like(rows_in)
    met = greet(
        [(around(head, k, heads), blk) for k in range(1, heads)]
        + [(head, around(blk, k, blks)) for k in range(1, blks)]
    )
    lanes = lane_ids((rows, LANES))
    for copy in fetched:
        copy.wait()
    rows_in[0:experts, 0:rows] = wr_ref[...].astype(F32)
    rows_in[experts : experts + 1, 0:rows] = g2_ref[...].astype(F32)
    rows_in[experts + 1 : experts + 2, 0:rows] = g1_ref[...].astype(F32)
    vectors = jnp.transpose(rows_in[...])[:rows]
    gain = vectors[:, experts + 1 : experts + 2]

    def columns(which):
        start = pl.multiple_of(which * model + head * LANES, LANES)
        return w_ref[:, pl.ds(start, LANES)].astype(F32) * gain

    key_cols = columns(1)
    value_cols = pltpu.roll(columns(2), HALF, 1)
    wall[blk, :, 0:LANES] = jnp.where(lanes < HALF, key_cols, value_cols).astype(BF16)
    wall[blk, :, LANES : 2 * LANES] = jnp.where(lanes < HALF, value_cols, key_cols).astype(BF16)
    wall[blk, :, 2 * LANES : 3 * LANES] = (columns(0) * HS ** (-0.5)).astype(BF16)
    def slice_copy(slot, source, target):
        ref = wall.at[source]
        return remote(ref, ref, w_send.at[slot], w_recv.at[source], head, target)

    pair = 2 * z + around(y, 1, 2)
    line = [2 * around(z, step, planes) + y for step in (1, planes - 1, *range(2, planes - 1))]
    w_copies = [slice_copy(slot, blk, target) for slot, target in enumerate((*line, pair))]
    w_onward = [slice_copy(planes + slot, source, pair) for slot, source in enumerate(line)]
    xhat, _ = centre(x_ref[...].astype(F32))
    xall[head] = xhat.astype(BF16)
    meet(met)
    for copy in w_copies:
        copy.start()
    x_copies = [
        remote(xall.at[head], xall.at[head], x_send.at[k], x_recv.at[k], around(head, k, heads), blk)
        for k in range(1, heads)
    ]
    for copy in x_copies:
        copy.start()
    wo_own[:, model : model + LANES] = vectors.astype(BF16)
    wo_all[blk, head] = wo_own[pl.ds(pl.multiple_of(head * part, part), part), :]
    o_copies = [
        remote(
            wo_all.at[blk, head], wo_all.at[blk, head],
            o_send.at[k], o_recv.at[k], head, around(blk, k, blks),
        )
        for k in range(1, blks)
    ]
    document_bounds(docs_ref, bounds, z)
    for source, copy in zip(line, w_onward):
        arrived(wall.at[source], w_recv.at[source])
        copy.start()
    for copy in o_copies:
        copy.start()
    for source in (pair, *[other - y + around(y, 1, 2) for other in line]):
        arrived(wall.at[source], w_recv.at[source])
    for copy in w_copies + w_onward:
        copy.wait_send()
    for copy in x_copies:
        copy.wait()
    weight = wall[...].reshape(model, 3 * LANES)
    tokens = x_ref.shape[0]
    even = y == 0
    above, below = z < planes - 1, z > 0
    half_span = kvall.shape[1] // 2
    sides = ((1, above, below, 0), (-1, below, above, 4))

    def half_of(ref, half):
        return ref.at[pl.ds(half * half_span, half_span)]

    def outward(slot, step, across, half):
        target = 2 * (z + step) + around(y, across, 2)
        return remote(
            half_of(kv_other if across else kvall.at[blk], half), half_of(kvall.at[blk], half),
            k_send.at[slot], k_recv.at[blk, half], head, target,
        )

    def onward(slot, step, side, half):
        from_span = 2 * (z - step) + side
        ref = half_of(kvall.at[from_span], half)
        return remote(ref, ref, k_send.at[slot], k_recv.at[from_span, half], head, 2 * (z + step) + y)

    def await_half(span, half):
        arrived(half_of(kvall.at[span], half), k_recv.at[span, half])

    def turn(span):
        size = kvall.shape[1]
        kvt[:, pl.ds(pl.multiple_of(span * size, size), size)] = jnp.transpose(kvall[span])

    for half in range(2):
        for piece in range(half * heads // 2, (half + 1) * heads // 2):
            made = dot(xall[piece], weight).astype(BF16)
            first, second = made[:, 0:LANES], made[:, LANES : 2 * LANES]
            span = slice(piece * tokens, (piece + 1) * tokens)
            kvall[blk, span, :] = jnp.where(even, first, second)
            kv_other[span, :] = jnp.where(even, second, first)
            qall[y, span, :] = made[:, 2 * LANES : 3 * LANES]
        outward(8 + half, 0, 1, half).start()
        for step, there, _, slot in sides:

            @pl.when(there)
            def _():
                outward(slot + 2 * half, step, 0, half).start()
                outward(slot + 2 * half + 1, step, 1, half).start()

    other_y = around(y, 1, 2)
    kept = (lane_ids(q_packed.shape) < HALF) == (y == 1)
    q_packed[...] = halves(qall[y].astype(F32), kept).astype(BF16)
    q_pair = remote(q_packed, q_landed, k_send.at[10], q_recv, head, 2 * z + other_y)
    q_pair.start()
    turn(blk)
    for copy in o_copies:
        copy.wait()
    core = lax.rem(head, 2)
    sibling, across = head - core + 1 - core, around(head, 2, heads)

    def quarter_copy(index, quarter, to_head):
        ref = wo_all.at[:, quarter]
        return remote(ref, ref, p_send.at[index], p_recv.at[index], to_head, blk)

    p_copies = [quarter_copy(0, head, sibling), quarter_copy(1, head, across)]
    for copy in p_copies:
        copy.start()
    p_copies.append(quarter_copy(2, across, sibling))
    for half in range(2):
        for step, there, back, slot in sides:

            @pl.when(back)
            def _():
                for side in range(2):
                    await_half(2 * (z - step) + side, half)

            @pl.when(jnp.logical_and(there, back))
            def _():
                for side in range(2):
                    onward(11 + slot + 2 * half + side, step, side, half).start()

    arrived(wo_all.at[:, across], p_recv.at[1])
    p_copies[2].start()
    for half in range(2):
        await_half(pair, half)
    turn(pair)
    q_pair.wait()
    landed = q_landed[...]
    qall[other_y, 0:half_span, :] = landed
    qall[other_y, half_span : 2 * half_span, :] = pltpu.roll(landed.astype(F32), HALF, 1).astype(BF16)
    key_tile = kvall.shape[1]
    for group in range(2 * key_tile // (CHAINS * QUERY_TILE)):
        tiles, queries = query_group(qall, group, y)
        carry = (nothing_attended(),) * CHAINS
        for side in range(2):
            first = pl.multiple_of((2 * z + side) * key_tile, key_tile)
            keys_across = kvt[:, pl.ds(first, key_tile)]
            carry = attend(bounds, tiles, first, kvall[2 * z + side], keys_across, queries, carry)
        for tile, (biggest, weight, mixed) in zip(tiles, carry):
            begun[tile, 0:LANES] = mixed
            begun[tile, LANES : LANES + 8] = jnp.broadcast_to(biggest, (8, QUERY_TILE))
            begun[tile, LANES + 8 : LANES + 16] = jnp.broadcast_to(weight, (8, QUERY_TILE))
    for step, there, back, slot in sides:

        @pl.when(back)
        def _():
            for side in range(2):
                turn(2 * (z - step) + side)

    for other in range(planes):
        for side in range(2):
            span = 2 * other + side

            @pl.when(jnp.logical_or(z - other == 2, other - z == 2))
            def _():
                for half in range(2):
                    await_half(span, half)
                turn(span)

    for index, quarter in ((0, sibling), (2, around(sibling, 2, heads))):
        arrived(wo_all.at[:, quarter], p_recv.at[index])
    for copy in p_copies:
        copy.wait_send()
    for half in range(2):
        outward(8 + half, 0, 1, half).wait_send()
        for step, there, back, slot in sides:

            @pl.when(there)
            def _():
                outward(slot + 2 * half, step, 0, half).wait_send()
                outward(slot + 2 * half + 1, step, 1, half).wait_send()

            @pl.when(jnp.logical_and(there, back))
            def _():
                for side in range(2):
                    onward(11 + slot + 2 * half + side, step, side, half).wait_send()


def document_bounds(docs_ref, bounds, z):
    count = docs_ref.shape[1]
    lengths = docs_ref[...].astype(F32)
    doc = lax.broadcasted_iota(jnp.int32, (count, count), 0)
    other = lane_ids((count, count))
    start = jnp.sum(jnp.where(other < doc, lengths, 0.0), axis=1, keepdims=True)
    end = jnp.sum(jnp.where(other <= doc, lengths, 0.0), axis=1, keepdims=True)
    queries = bounds.shape[1]
    token = (z * queries + lane_ids((count, queries))).astype(F32)
    begun = start <= token
    bounds[...] = jnp.zeros_like(bounds)
    bounds[0:1, :] = jnp.max(jnp.where(begun, start, 0.0), axis=0, keepdims=True).astype(jnp.int32)
    bounds[1:2, :] = jnp.max(jnp.where(begun, end, 0.0), axis=0, keepdims=True).astype(jnp.int32)


def vmem_specs(count):
    return [pl.BlockSpec(memory_space=pltpu.VMEM)] * count


def hbm_specs(count):
    return [pl.BlockSpec(memory_space=pltpu.HBM)] * count


def in_hbm(*arrays):
    return [pltpu.with_memory_space_constraint(array, pltpu.HBM) for array in arrays]


def dma(*shape):
    return pltpu.SemaphoreType.DMA(shape)


def call_qkv(x, w_qkv, g1, w_out, w_router, g2, doc_lengths, heads, blks):
    tokens, model = x.shape
    rows = w_qkv.shape[0]
    span = tokens * heads
    wide = model + LANES
    part = rows // heads
    return pl.pallas_call(
        functools.partial(qkv_kernel, heads, blks),
        out_shape=(
            jax.ShapeDtypeStruct((2, span, LANES), BF16),
            jax.ShapeDtypeStruct((blks, span, LANES), BF16),
            jax.ShapeDtypeStruct((heads, tokens, model), BF16),
            jax.ShapeDtypeStruct((blks, rows, 3 * LANES), BF16),
            jax.ShapeDtypeStruct((blks, heads, part, wide), BF16),
            jax.ShapeDtypeStruct((LANES, blks * span), BF16),
            jax.ShapeDtypeStruct((8, 2 * span), jnp.int32),
            jax.ShapeDtypeStruct((2 * span // QUERY_TILE, LANES + 16, QUERY_TILE), F32),
        ),
        in_specs=hbm_specs(7),
        out_specs=tuple(vmem_specs(8)),
        scratch_shapes=[
            pltpu.VMEM((tokens, model), BF16),
            pltpu.VMEM((rows, 3 * model), BF16),
            pltpu.VMEM((LANES, LANES), F32),
            pltpu.VMEM((1, rows), BF16),
            pltpu.VMEM((1, rows), BF16),
            pltpu.VMEM((w_router.shape[1], rows), BF16),
            pltpu.VMEM((1, doc_lengths.shape[0]), jnp.int32),
            pltpu.VMEM((rows, wide), BF16),
            pltpu.VMEM((span, LANES), BF16),
            pltpu.VMEM((span // 2, LANES), BF16),
            pltpu.VMEM((span // 2, LANES), BF16),
            dma(7),
            dma(heads), dma(heads), dma(blks), dma(blks), dma(blks), dma(blks), dma(heads), dma(heads),
            dma(19), dma(blks, 2), pltpu.SemaphoreType.DMA,
        ],
        compiler_params=pltpu.CompilerParams(
            collective_id=1, has_side_effects=True, vmem_limit_bytes=16 * MIB
        ),
        name="qkv",
    )(
        *in_hbm(
            x, w_qkv, g1.reshape(1, rows), w_out, w_router.T, g2.reshape(1, rows),
            doc_lengths.reshape(1, -1),
        )
    )


def other_blocks(bounds_ref, group, key_tile, z, step, carry):
    low, high = group_blocks(bounds_ref, group, CHAINS * QUERY_TILE, key_tile)
    carry = lax.fori_loop(low, 2 * z, step, carry)
    return lax.fori_loop(2 * z + 2, high, step, carry)


def forward_kernel(bounds_ref, q_ref, kv_ref, kvt_ref, begun_ref, o_out, ob_out, lse_out):
    _, _, z, y = place()
    key_tile = kv_ref.shape[1]
    value_lanes = (lane_ids((HALF, LANES)) < HALF) == (y == 1)
    for group in range(q_ref.shape[0] * q_ref.shape[1] // (CHAINS * QUERY_TILE)):
        tiles, queries = query_group(q_ref, group, y)

        def step(block, carry, queries=queries, tiles=tiles):
            first = pl.multiple_of(block * key_tile, key_tile)
            across = kvt_ref[:, pl.ds(first, key_tile)]
            return attend(bounds_ref, tiles, first, kv_ref[block], across, queries, carry)

        start = tuple(
            (begun_ref[t, LANES : LANES + 1], begun_ref[t, LANES + 8 : LANES + 9], begun_ref[t, 0:LANES])
            for t in tiles
        )
        ends = other_blocks(bounds_ref, group, key_tile, z, step, start)
        for tile, (biggest, weight, mixed) in zip(tiles, ends):
            result = jnp.transpose(mixed / weight)
            o_out[tile] = result
            for part in range(QUERY_TILE // LANES):
                block = result[part * LANES : (part + 1) * LANES]
                ob_out[tile, part] = halves(block, value_lanes).astype(BF16)
            lse_out[tile] = jnp.broadcast_to(biggest + jnp.log(weight), (8, QUERY_TILE))


def call_forward(bounds, q, kv, kvt, begun):
    blks, span, _ = kv.shape
    tiles = 2 * span // QUERY_TILE
    return pl.pallas_call(
        forward_kernel,
        out_shape=(
            jax.ShapeDtypeStruct((tiles, QUERY_TILE, LANES), F32),
            jax.ShapeDtypeStruct((tiles, QUERY_TILE // LANES, HALF, LANES), BF16),
            jax.ShapeDtypeStruct((tiles, 8, QUERY_TILE), F32),
        ),
        in_specs=vmem_specs(5),
        out_specs=tuple(vmem_specs(3)),
        compiler_params=pltpu.CompilerParams(vmem_limit_bytes=16 * MIB),
        name="attend",
    )(bounds, q, kv, kvt, begun)


def backward_kernel(
    bounds_ref, q_ref, kv_ref, kvt_ref, do_ref, o_ref, lse_ref, dq_out, dkv_out, delta_out, dkv
):
    _, _, z, y = place()
    key_tile = kv_ref.shape[1]
    dkv[...] = jnp.zeros_like(dkv)
    for group in range(q_ref.shape[0] * q_ref.shape[1] // (CHAINS * QUERY_TILE)):
        tiles, queries = query_group(q_ref, group, y)
        out_grads = group_grads(do_ref, tiles, y)
        deltas, log_totals = [], []
        for tile, out_grad in zip(tiles, out_grads):
            product = jnp.transpose(out_grad.astype(F32) * o_ref[tile])
            deltas.append(jnp.sum(product, axis=0, keepdims=True))
            delta_out[tile] = jnp.broadcast_to(deltas[-1], delta_out.shape[1:])
            log_totals.append(lse_ref[tile, 0:1, :])
        known = (queries, out_grads, deltas, log_totals)

        def step(block, carry, tiles=tiles, known=known):
            first = pl.multiple_of(block * key_tile, key_tile)
            across = kvt_ref[:, pl.ds(first, key_tile)]
            given, carry = attend_back(bounds_ref, tiles, first, kv_ref[block], across, known, carry)
            dkv[block] += given
            return carry

        zero = jnp.zeros((LANES, QUERY_TILE), F32)
        ends = other_blocks(bounds_ref, group, key_tile, z, step, (zero,) * CHAINS)
        for tile, mixed in zip(tiles, ends):
            dq_out[tile] = mixed
    for block in range(dkv.shape[0]):
        dkv_out[block] = dkv[block].astype(BF16)


def call_backward(bounds, q, kv, kvt, d_o, o, lse):
    blks, span, _ = kv.shape
    tiles = 2 * span // QUERY_TILE
    return pl.pallas_call(
        backward_kernel,
        out_shape=(
            jax.ShapeDtypeStruct((tiles, LANES, QUERY_TILE), F32),
            jax.ShapeDtypeStruct((blks, span, LANES), BF16),
            jax.ShapeDtypeStruct((tiles, 8, QUERY_TILE), F32),
        ),
        in_specs=vmem_specs(7),
        out_specs=tuple(vmem_specs(3)),
        scratch_shapes=[pltpu.VMEM((blks, span, LANES), F32)],
        compiler_params=pltpu.CompilerParams(vmem_limit_bytes=16 * MIB),
        name="attend_back",
    )(bounds, q, kv, kvt, d_o, o, lse)


def gelu_parts(values):
    share = 0.5 * (1.0 + lax.erf(values * (2.0**-0.5)))
    slope = share + values * jnp.exp(-0.5 * values * values) * (2.0 * math.pi) ** -0.5
    return values * share, slope


def positions(expert_rows, expert_cols, rank_row, rank_col):
    def count(mask, axis):
        return jnp.sum(mask.astype(F32), axis=axis, keepdims=True)

    row = [None, None]
    col = [None, None]
    before = rank_col < rank_row
    after = rank_row < rank_col
    for choice in range(2):
        row[choice] = count((expert_cols[choice] == expert_rows[choice]) & before, 0)
        col[choice] = count((expert_rows[choice] == expert_cols[choice]) & after, 1)
    row[1] = row[1] + count(expert_cols[0] == expert_rows[1], 0)
    col[1] = col[1] + count(expert_rows[0] == expert_cols[1], 1)
    return row, col


def own_columns(rows_ref, turned, blk, capacity):
    blks, _, slots = rows_ref.shape
    rows = jnp.concatenate(
        [rows_ref[...].reshape(blks, slots), jnp.zeros((LANES - blks, slots), F32)], axis=0
    )
    for piece in range(slots // LANES):
        columns = slice(piece * LANES, (piece + 1) * LANES)
        turned[columns, :] = jnp.transpose(rows[:, columns])
    own = turned[pl.ds(pl.multiple_of(blk * capacity, capacity), capacity), :]
    return jnp.concatenate([own[:, source : source + 1] for source in range(blks)], axis=0)


def middle_kernel(
    heads, blks,
    x_hbm, o_ref, wo_ref, routes_hbm, rank_hbm, d_out_hbm, win_hbm, wout_hbm,
    po, pa, hidden_ref, share_ref, dh_ref, dma_all, grads_ref, rx,
    x_ref, routes_ref, rank_ref, d_out_ref, win_ref, wout_ref, rows_in, in_sem,
    o_all, dos, doa, rs, ra, dr, da, dms, acc_out, acc_row, mix, gate_rows, d_gate_rows, turned,
    o_send, o_recv, dos_send, dos_recv, r_send, r_recv,
    dr_send, dr_recv, dm_send, dm_recv, rx_send, rx_recv, g_send, g_recv, dg_send, dg_recv, pa_send, pa_recv,
):
    head, blk, z, y = place()
    tokens, model = x_ref.shape
    capacity = 2 * tokens // blks
    slots = capacity * blks
    plane = [(k % heads, k // heads) for k in range(1, 2 * heads)]
    wanted = (
        (routes_hbm, routes_ref), (rank_hbm, rank_ref), (d_out_hbm, d_out_ref), (x_hbm, x_ref),
        (win_hbm, win_ref), (wout_hbm, wout_ref),
    )
    fetched = [
        pltpu.make_async_copy(src, dst, in_sem.at[i]) for i, (src, dst) in enumerate(wanted)
    ]
    for copy in fetched:
        copy.start()
    met = greet(
        [(around(head, kh, heads), 2 * z + around(y, ky, 2)) for kh, ky in plane]
        + [(head, around(blk, k, blks)) for k in range(1, blks)]
    )
    meet(met)

    def plane_copies(src_of, dst, send, recv):
        copies = []
        for k, (kh, ky) in enumerate(plane):
            to_head, to_y = around(head, kh, heads), around(y, ky, 2)
            copies.append(
                remote(src_of(to_y, to_head), dst, send.at[k], recv.at[k], to_head, 2 * z + to_y)
            )
        return copies

    def blk_copies(src, dst, send, recv):
        return [
            remote(
                src.at[around(blk, k, blks)], dst.at[blk],
                send.at[k], recv.at[k], head, around(blk, k, blks),
            )
            for k in range(1, blks)
        ]

    def start(copies):
        for copy in copies:
            copy.start()

    def finish(copies):
        for copy in copies:
            copy.wait()

    o_copies = plane_copies(lambda to_y, to_head: o_ref.at[to_y, to_head], o_all.at[y, head], o_send, o_recv)
    start(o_copies)
    o_all[y, head] = o_ref[y, head]

    lanes = lane_ids((tokens, LANES))
    for copy in fetched[:4]:
        copy.wait()
    e_rows = [routes_ref[i : i + 1, :].astype(F32) for i in range(2)]
    rank_row = rank_ref[...].astype(F32)
    rows_in[...] = jnp.zeros_like(rows_in)
    rows_in[0:1, :], rows_in[1:2, :], rows_in[2:3, :] = *e_rows, rank_row
    columns = jnp.transpose(rows_in[...])
    e_cols = [columns[:, 0:1], columns[:, 1:2]]
    rank_col = columns[:, 2:3]
    pos_rows, pos_cols = positions(e_rows, e_cols, rank_row, rank_col)

    def slot_of(expert, position):
        return jnp.where(position < capacity, expert * capacity + position, -1.0).astype(jnp.int32)

    slot_rows = [slot_of(e, p) for e, p in zip(e_rows, pos_rows)]
    slot_cols = [slot_of(e, p) for e, p in zip(e_cols, pos_cols)]
    slot_down = lax.broadcasted_iota(jnp.int32, (slots, tokens), 0)
    slot_across = lane_ids((tokens, slots))
    pick = [(slot_down == s).astype(BF16) for s in slot_rows]
    put = [(slot_across == s).astype(BF16) for s in slot_cols]
    pick_any = pick[0] + pick[1]
    put_any = put[0] + put[1]

    d_out = d_out_ref[...]
    dos[...] = dot(pick_any, d_out.astype(BF16)).astype(BF16).reshape(dos.shape)
    dos_copies = blk_copies(dos, doa, dos_send, dos_recv)
    start(dos_copies)
    doa[blk] = dos[blk]

    weight_out = jnp.concatenate(
        [wo_ref[(b ^ 1) * HALF : ((b ^ 1) + 1) * HALF, 0:model] for b in range(blks)], axis=0
    )
    small = wo_ref[:, model : model + LANES]
    small_across = jnp.concatenate(
        [
            jnp.transpose(small[i * LANES : (i + 1) * LANES].astype(F32))
            for i in range(model // LANES)
        ],
        axis=1,
    )
    gain = small_across[blks : blks + 1, :]

    finish(o_copies)
    low_lanes = lanes[:HALF] < HALF
    for piece in range(heads):
        columns = slice(piece * LANES, (piece + 1) * LANES)
        first, second = o_all[1, piece].astype(F32), o_all[0, piece].astype(F32)
        mix[:HALF, columns] = jnp.where(low_lanes, first, second).astype(BF16)
        swapped = pltpu.roll(jnp.where(low_lanes, second, first), HALF, 1)
        mix[HALF:, columns] = swapped.astype(BF16)
    mixed = mix[...]
    hidden = x_ref[...].astype(F32) + dot(mixed, weight_out)
    xhat, scale = centre(hidden)
    routed = (xhat * gain).astype(BF16)
    rs[...] = dot(pick_any, routed).astype(BF16).reshape(rs.shape)
    r_copies = blk_copies(rs, ra, r_send, r_recv)
    start(r_copies)
    ra[blk] = rs[blk]
    logits = jnp.where(lanes < blks, dot(routed, small), MASKED)
    powers = jnp.exp(logits - jnp.max(logits, axis=1, keepdims=True))
    probs = powers / jnp.sum(powers, axis=1, keepdims=True)
    lanes_f = lanes.astype(F32)
    hots = [lanes_f == e for e in e_cols]
    gates = [jnp.sum(jnp.where(hot, probs, 0.0), axis=1, keepdims=True) for hot in hots]
    gate_high = [g.astype(BF16).astype(F32) for g in gates]
    gate_across = jnp.transpose(
        jnp.where(lanes == 0, gate_high[0], jnp.where(lanes == 1, gates[0] - gate_high[0], 0.0))
        + jnp.where(lanes == 2, gate_high[1], jnp.where(lanes == 3, gates[1] - gate_high[1], 0.0))
    ).astype(BF16)
    by_slot = (dot(gate_across, put[0]), dot(gate_across, put[1]))
    gate_rows[blk] = by_slot[0][0:1] + by_slot[0][1:2] + by_slot[1][2:3] + by_slot[1][3:4]
    g_copies = [
        remote(
            gate_rows.at[blk], gate_rows.at[blk],
            g_send.at[k], g_recv.at[k], head, around(blk, k, blks),
        )
        for k in range(1, blks)
    ]
    start(g_copies)
    acc_out[...] = jnp.zeros_like(acc_out)
    acc_row[...] = jnp.zeros_like(acc_row)
    finish(dos_copies)
    finish(r_copies)

    out_rows = doa[...].reshape(slots, model)
    rx[head, :, 0:model] = ra[...].reshape(slots, model)
    finish(g_copies)
    gate_col = own_columns(gate_rows, turned, blk, capacity)
    rx[head, :, model : 2 * model] = (out_rows.astype(F32) * gate_col).astype(BF16)
    core = lax.rem(head, 2)
    sibling, across = head - core + 1 - core, around(head, 2, heads)

    def half_rows(source, half):
        return rx.at[source, pl.ds(half * slots // 2, slots // 2)]

    to_across = [
        remote(
            half_rows(head, half), half_rows(head, half),
            rx_send.at[1 + half], rx_recv.at[1 + half], across, blk,
        )
        for half in range(2)
    ]
    to_sibling = remote(rx.at[head], rx.at[head], rx_send.at[0], rx_recv.at[0], sibling, blk)
    forwards = [
        remote(
            half_rows(across, half), half_rows(across, half),
            rx_send.at[3 + half], rx_recv.at[3 + half], sibling, blk,
        )
        for half in range(2)
    ]
    start(to_across)
    to_sibling.start()
    half_ff = wout_ref.shape[0] // 4
    for copy in fetched[4:]:
        copy.wait()

    @pl.loop(0, 4)
    def _(chunk):
        first = pl.multiple_of(chunk * half_ff, half_ff)
        into = win_ref[:, pl.ds(first, half_ff)]
        outof = wout_ref[pl.ds(first, half_ff), :]
        act, slope = gelu_parts(dot(rx[head, :, 0:model], into))
        acc_out[...] += dot(act.astype(BF16), outof)
        d_act = dot(rx[head, :, model : 2 * model], outof, (1, 1))
        acc_row[...] += dot((slope * d_act).astype(BF16), into, (1, 1))

    result = acc_out[...].astype(BF16)
    d_gate = jnp.sum(out_rows.astype(F32) * result.astype(F32), axis=1, keepdims=True)
    dr[...] = acc_row[...].astype(BF16).reshape(dr.shape)
    dr_copies = blk_copies(dr, da, dr_send, dr_recv)
    start(dr_copies)
    da[blk] = dr[blk]
    d_wide = jnp.broadcast_to(d_gate, (slots, LANES))
    d_gate_rows[blk] = jnp.concatenate(
        [jnp.transpose(d_wide[i * LANES : (i + 1) * LANES])[0:1] for i in range(slots // LANES)],
        axis=1,
    )
    dg_copies = [
        remote(
            d_gate_rows.at[blk], d_gate_rows.at[blk],
            dg_send.at[k], dg_recv.at[k], head, around(blk, k, blks),
        )
        for k in range(1, blks)
    ]
    start(dg_copies)
    po[...] = result.reshape(blks, capacity, model)

    finish(dg_copies)
    back_gate = own_columns(d_gate_rows, turned, blk, capacity)
    back_gate = split_high_low(back_gate, lane_ids((slots, LANES)))
    d_gates = [join_high_low(dot(p, back_gate), 0) for p in put]
    d_probs = jnp.where(hots[0], d_gates[0], 0.0) + jnp.where(hots[1], d_gates[1], 0.0)
    d_logits = probs * (d_probs - jnp.sum(probs * d_probs, axis=1, keepdims=True))
    d_high = d_logits.astype(BF16)
    d_low = (d_logits - d_high.astype(F32)).astype(BF16)
    d_router_part = dot(d_high, small, (1, 1)) + dot(d_low, small, (1, 1))
    finish(dr_copies)
    d_routed = dot(put_any, da[...].reshape(slots, model)) + d_router_part
    d_hidden = d_out + centre_back(d_routed * gain, xhat, scale)
    dh_ref[...] = d_hidden
    d_attn = d_hidden.astype(BF16)
    d_mixed = dot(d_attn, weight_out, (1, 1))
    for piece in range(heads):
        block = d_mixed[:, piece * LANES : (piece + 1) * LANES]
        for to_y in range(2):
            dms[to_y, piece] = halves(block, low_lanes == (to_y == 1)).astype(BF16)
    dm_copies = plane_copies(lambda to_y, to_head: dms.at[to_y, to_head], dma_all.at[y, head], dm_send, dm_recv)
    start(dm_copies)
    dma_all[y, head] = dms[y, head]
    first_half = pa.shape[1]
    pa_copies = [
        remote(
            po.at[around(blk, k, blks), pl.ds(0, first_half)], pa.at[blk],
            pa_send.at[k], pa_recv.at[k], head, around(blk, k, blks),
        )
        for k in range(1, blks)
    ]
    start(pa_copies)
    pa[blk] = po[blk, 0:first_half]
    arrived(half_rows(across, 0), rx_recv.at[1])
    forwards[0].start()

    d_weight = dot(mixed, d_attn, (0, 0)).astype(BF16)
    for b in range(blks):
        grads_ref[b, :, 0:model] = d_weight[(b ^ 1) * HALF : ((b ^ 1) + 1) * HALF, :]
    last = (lanes == blks).astype(BF16)
    d_small = dot(routed, d_high, (0, 0)) + dot((d_routed * xhat).astype(BF16), last, (0, 0))
    grads_ref[:, :, model : model + LANES] = d_small.astype(BF16).reshape(blks, HALF, LANES)
    share = gates[0] * put[0].astype(F32) + gates[1] * put[1].astype(F32)
    share_ref[0] = share.astype(BF16)
    share_ref[1] = (share - share_ref[0].astype(F32)).astype(BF16)
    hidden_ref[...] = hidden

    arrived(half_rows(across, 1), rx_recv.at[2])
    forwards[1].start()
    finish(dm_copies)
    finish(pa_copies)
    to_sibling.wait()
    for copy in to_across:
        copy.wait_send()
    finish(forwards)


def call_middle(x, o, wo, routes, rank, d_out, win, wout, heads, blks):
    tokens, model = x.shape
    capacity = 2 * tokens // blks
    slots = capacity * blks
    wide = model + LANES

    def rows(width):
        return pltpu.VMEM((blks, capacity, width), BF16)

    def block(*lead):
        return pltpu.VMEM((*lead, tokens // 2, LANES), BF16)

    return pl.pallas_call(
        functools.partial(middle_kernel, heads, blks),
        out_shape=(
            jax.ShapeDtypeStruct((blks, capacity, model), BF16),
            jax.ShapeDtypeStruct((blks, capacity // 2, model), BF16),
            jax.ShapeDtypeStruct((tokens, model), F32),
            jax.ShapeDtypeStruct((2, tokens, slots), BF16),
            jax.ShapeDtypeStruct((tokens, model), F32),
            jax.ShapeDtypeStruct((2, heads, tokens // 2, LANES), BF16),
            jax.ShapeDtypeStruct((blks, model // blks, wide), BF16),
            jax.ShapeDtypeStruct((heads, slots, 2 * model), BF16),
        ),
        in_specs=hbm_specs(1) + vmem_specs(2) + hbm_specs(5),
        out_specs=tuple(vmem_specs(8)),
        scratch_shapes=[
            pltpu.VMEM((tokens, model), BF16),
            pltpu.VMEM((2, tokens), jnp.int32),
            pltpu.VMEM((1, tokens), jnp.int32),
            pltpu.VMEM((tokens, model), F32),
            pltpu.VMEM(win.shape, BF16),
            pltpu.VMEM(wout.shape, BF16),
            pltpu.VMEM((tokens, tokens), F32),
            dma(6),
            block(2, heads), rows(model), rows(model), rows(model), rows(model),
            rows(model), rows(model), block(2, heads),
            pltpu.VMEM((slots, model), F32), pltpu.VMEM((slots, model), F32),
            pltpu.VMEM((tokens, model), BF16),
            pltpu.VMEM((blks, 1, slots), F32), pltpu.VMEM((blks, 1, slots), F32),
            pltpu.VMEM((slots, LANES), F32),
            dma(2 * heads), dma(2 * heads), dma(blks), dma(blks), dma(blks), dma(blks),
            dma(blks), dma(blks), dma(2 * heads), dma(2 * heads), dma(5), dma(5),
            dma(blks), dma(blks), dma(blks), dma(blks), dma(blks), dma(blks),
        ],
        compiler_params=pltpu.CompilerParams(
            collective_id=2, has_side_effects=True, vmem_limit_bytes=20 * MIB
        ),
        name="experts",
    )(*in_hbm(x), o, wo, *in_hbm(routes.T, rank, d_out, win, wout))


def last_kernel(
    heads, blks,
    x_hbm, dh_ref, begun_ref, dkv_ref, xa_ref, wa_ref, w_hbm, g1_hbm, grads_ref, rx_ref, win_hbm, wout_hbm,
    po_ref, pa_ref, hidden_ref, share_ref, bounds_ref, q_ref, kv_ref, kvt_ref, do_ref, lse_ref, delta_ref,
    y_ref, dx_ref, dw_ref, shared_ref, din_ref, dout_ref,
    x_ref, w_ref, g1_ref, win_ref, wout_ref, in_sem,
    gain_tile, far_all, near_send_buf, near_all, pair_all, dq_all, dq_ref, dq_packed, dkv_own, pair_buf, us, ua, gs, ga, gqs, gqa, u_part, xat, pa, gh, ghq, w1, w2s, w2, w3,
    q_send, q_recv, pair_send, pair_recv, far_send, far_recv, near_send, near_recv,
    u_send, u_recv, g_send, g_recv, gh_send, gh_recv, w1_send, w1_recv, w2_send, w2_recv,
    w3_send, w3_recv, e_send, e_recv, gq_send, gq_recv, po_send, po_recv, ghq_send, ghq_recv,
    din_half, dout_half,
):
    head, blk, z, y = place()
    planes = blks // 2
    tokens, model = x_ref.shape
    rows = w_ref.shape[0]
    wanted = (
        (win_hbm, win_ref), (wout_hbm, wout_ref), (x_hbm, x_ref), (w_hbm, w_ref), (g1_hbm, g1_ref)
    )
    fetched = [
        pltpu.make_async_copy(src, dst, in_sem.at[i]) for i, (src, dst) in enumerate(wanted)
    ]
    for copy in fetched:
        copy.start()
    met = greet(
        [(around(head, k, heads), blk) for k in range(1, heads)]
        + [(head, around(blk, k, blks)) for k in range(1, blks)]
    )
    meet(met)

    def start(copies):
        for copy in copies:
            copy.start()

    def finish(copies):
        for copy in copies:
            copy.wait()

    other_y = around(y, 1, 2)
    pair = 2 * z + other_y
    above, below = z < planes - 1, z > 0
    directions = ((1, above, below, 0), (-1, below, above, 2))

    half_span = dkv_ref.shape[1] // 2

    def half_of(ref, half):
        return ref.at[pl.ds(half * half_span, half_span)]

    def far_copy(step, slot, side, half):
        span = 2 * (z + 2 * step) + side
        return remote(
            half_of(dkv_ref.at[span], half), half_of(far_all.at[slot + side], half),
            far_send.at[slot + side, half], far_recv.at[slot + side, half], head, 2 * (z + step) + y,
        )

    def near_copy(step, slot, side, half):
        return remote(
            half_of(near_send_buf.at[slot + side], half), half_of(near_all.at[slot // 2, y], half),
            near_send.at[slot + side, half], near_recv.at[slot // 2, y, half],
            head, 2 * (z + step) + side,
        )

    def two_away(step):
        return z + 2 * step < planes if step > 0 else z + 2 * step >= 0

    for half in range(2):
        for step, there, back, slot in directions:

            @pl.when(two_away(step))
            def _():
                for side in range(2):
                    far_copy(step, slot, side, half).start()

    w1_copies = [
        remote(
            grads_ref.at[:, around(head, k, heads)], w1.at[head],
            w1_send.at[k], w1_recv.at[k], around(head, k, heads), blk,
        )
        for k in range(1, heads)
    ]
    start(w1_copies)
    w1[head] = grads_ref[:, head]

    core = lax.rem(head, 2)
    sibling = head - core + 1 - core
    ff_half = wout_ref.shape[0] // 2
    ff_step = ff_half // 4

    def expert_chunk(chunk):
        here = pl.multiple_of(core * ff_half + chunk * ff_step, ff_step)
        there = pl.multiple_of(chunk * ff_step, ff_step)
        into = win_ref[:, pl.ds(here, ff_step)]
        outof = wout_ref[pl.ds(here, ff_step), :]
        d_in = jnp.zeros((model, ff_step), F32)
        d_out = jnp.zeros((ff_step, model), F32)
        for source in range(heads):
            rows_in = rx_ref[source, :, 0:model]
            grads_out = rx_ref[source, :, model : 2 * model]
            act, slope = gelu_parts(dot(rows_in, into))
            d_act = dot(grads_out, outof, (1, 1))
            d_in = d_in + dot(rows_in, (slope * d_act).astype(BF16), (0, 0))
            d_out = d_out + dot(act.astype(BF16), grads_out, (0, 0))
        din_ref[:, pl.ds(here, ff_step)] = d_in
        dout_ref[pl.ds(here, ff_step), :] = d_out
        din_half[core, :, pl.ds(there, ff_step)] = d_in.astype(BF16)
        dout_half[core, pl.ds(there, ff_step), :] = d_out.astype(BF16)

    key_tile = kv_ref.shape[1]
    for group in range(2 * key_tile // (CHAINS * QUERY_TILE)):
        tiles, queries = query_group(q_ref, group, y)
        known = (
            queries,
            group_grads(do_ref, tiles, y),
            [delta_ref[tile, 0:1, :] for tile in tiles],
            [lse_ref[tile, 0:1, :] for tile in tiles],
        )
        carry = tuple(begun_ref[tile] for tile in tiles)
        for side in range(2):
            first = pl.multiple_of((2 * z + side) * key_tile, key_tile)
            keys_across = kvt_ref[:, pl.ds(first, key_tile)]
            given, carry = attend_back(
                bounds_ref, tiles, first, kv_ref[2 * z + side], keys_across, known, carry
            )
            dkv_own[side] = given if group == 0 else dkv_own[side] + given
        for tile, total in zip(tiles, carry):
            at = tile * QUERY_TILE % key_tile
            dq_ref[tile * QUERY_TILE // key_tile, at : at + QUERY_TILE] = jnp.transpose(total)
    pair_buf[...] = dkv_own[other_y].astype(BF16)
    pair_copy = remote(pair_buf, pair_all, pair_send, pair_recv, head, pair)
    pair_copy.start()
    own_lanes = (lane_ids(dq_packed.shape) < HALF) == (y == 0)
    dq_packed[...] = halves(dq_ref[other_y], own_lanes).astype(BF16)
    q_copy = remote(dq_packed, dq_all, q_send, q_recv, head, pair)
    q_copy.start()
    for half in range(2):
        rows_here = slice(half * half_span, (half + 1) * half_span)
        for step, there, back, slot in directions:

            @pl.when(there)
            def _():
                for side in range(2):
                    near_send_buf[slot + side, rows_here] = dkv_ref[2 * (z + step) + side, rows_here]

            @pl.when(jnp.logical_and(there, back))
            def _():
                for side in range(2):
                    arrived(half_of(far_all.at[slot + side], half), far_recv.at[slot + side, half])
                    near_send_buf[slot + side, rows_here] = (
                        near_send_buf[slot + side, rows_here].astype(F32)
                        + far_all[slot + side, rows_here].astype(F32)
                    ).astype(BF16)

            @pl.when(there)
            def _():
                for side in range(2):
                    near_copy(step, slot, side, half).start()

    finish(fetched[:2])
    weight = wa_ref[...].reshape(model, 3 * LANES)
    for piece in range(heads):
        xat[:, piece * tokens : (piece + 1) * tokens] = jnp.transpose(xa_ref[piece])
    even = y == 0


    @pl.loop(0, 2)
    def _(chunk):
        expert_chunk(chunk)

    q_copy.wait()
    landed = dq_all[...].astype(F32)
    landed = jnp.concatenate([landed, pltpu.roll(landed, HALF, 1)], axis=0)
    own_lanes = (lane_ids(landed.shape) < HALF) == even
    q_grads = jnp.where(own_lanes, dq_ref[y], landed).astype(BF16)
    gqs[...] = dot(xat[...], q_grads).astype(BF16).reshape(gqs.shape)
    gq_copies = [
        remote(
            gqs.at[around(blk, k, blks)], gqa.at[blk],
            gq_send.at[k], gq_recv.at[k], head, around(blk, k, blks),
        )
        for k in range(1, blks)
    ]
    start(gq_copies)
    gqa[blk] = gqs[blk]
    u_part[...] = dot(q_grads, weight[:, 2 * LANES : 3 * LANES], (1, 1)).reshape(u_part.shape)

    finish(w1_copies)
    summed = w1[0].astype(F32)
    for source in range(1, heads):
        summed = summed + w1[source].astype(F32)
    w2s[...] = summed.astype(BF16)
    w2_copies = [
        remote(
            w2s.at[around(blk, k, blks)], w2.at[blk],
            w2_send.at[k], w2_recv.at[k], head, around(blk, k, blks),
        )
        for k in range(1, blks)
    ]
    start(w2_copies)
    w2[blk] = w2s[blk]

    @pl.loop(2, 4)
    def _(chunk):
        expert_chunk(chunk)

    e_copies = [
        remote(din_half.at[core], din_half.at[core], e_send.at[0], e_recv.at[0], sibling, blk),
        remote(dout_half.at[core], dout_half.at[core], e_send.at[1], e_recv.at[1], sibling, blk),
    ]
    start(e_copies)

    pair_copy.wait()
    for step, there, back, slot in directions:

        @pl.when(back)
        def _():
            for side in range(2):
                for half in range(2):
                    arrived(
                        half_of(near_all.at[slot // 2, side], half),
                        near_recv.at[slot // 2, side, half],
                    )

        @pl.when(jnp.logical_not(back))
        def _():
            near_all[slot // 2] = jnp.zeros(near_all.shape[1:], BF16)

    own = dkv_own[y]
    other = pair_all[...].astype(F32)
    made = jnp.concatenate(
        [
            (
                jnp.where(even == (side == 0), own, other)
                + near_all[0, side].astype(F32)
                + near_all[1, side].astype(F32)
            ).astype(BF16)
            for side in range(2)
        ],
        axis=1,
    )
    gs[...] = dot(xat[...], made).astype(BF16).reshape(gs.shape)
    g_copies = [
        remote(
            gs.at[around(blk, k, blks)], ga.at[blk],
            g_send.at[k], g_recv.at[k], head, around(blk, k, blks),
        )
        for k in range(1, blks)
    ]
    start(g_copies)
    ga[blk] = gs[blk]
    us[...] = (
        u_part[...] + dot(made, weight[:, 0 : 2 * LANES], (1, 1)).reshape(us.shape)
    ).astype(BF16)
    u_copies = [
        remote(
            us.at[around(head, k, heads)], ua.at[head],
            u_send.at[k], u_recv.at[k], around(head, k, heads), blk,
        )
        for k in range(1, heads)
    ]
    start(u_copies)
    ua[head] = us[head]
    finish(fetched[2:])
    finish(gq_copies)
    total = gqa[0].astype(F32)
    for source in range(1, blks):
        total = total + gqa[source].astype(F32)
    ghq[head] = total.astype(BF16)
    ghq_copies = [
        remote(ghq.at[head], ghq.at[head], ghq_send.at[k], ghq_recv.at[k], around(head, k, heads), blk)
        for k in range(1, heads)
    ]
    start(ghq_copies)

    finish(w2_copies)
    part = w2[0].astype(F32)
    for source in range(1, blks):
        part = part + w2[source].astype(F32)
    w3[head] = part.astype(BF16)
    w3_copies = [
        remote(w3.at[head], w3.at[head], w3_send.at[k], w3_recv.at[k], around(head, k, heads), blk)
        for k in range(1, heads)
    ]
    start(w3_copies)

    xhat, scale = centre(x_ref[...].astype(F32))
    finish(e_copies)
    there = pl.multiple_of((1 - core) * ff_half, ff_half)
    din_ref[:, pl.ds(there, ff_half)] = din_half[1 - core].astype(F32)
    dout_ref[pl.ds(there, ff_half), :] = dout_half[1 - core].astype(F32)
    finish(g_copies)
    total = ga[0].astype(F32)
    for source in range(1, blks):
        total = total + ga[source].astype(F32)
    gh[head] = total.astype(BF16)
    gh_copies = [
        remote(gh.at[head], gh.at[head], gh_send.at[k], gh_recv.at[k], around(head, k, heads), blk)
        for k in range(1, heads)
    ]
    start(gh_copies)
    half_slots = pa_ref.shape[1]
    po_copies = [
        remote(
            po_ref.at[around(blk, k, blks), pl.ds(half_slots, half_slots)], pa.at[blk],
            po_send.at[k], po_recv.at[k], head, around(blk, k, blks),
        )
        for k in range(1, blks)
    ]
    start(po_copies)
    pa[blk] = po_ref[blk, half_slots : 2 * half_slots]
    finish(u_copies)
    grad = ua[0].astype(F32)
    for source in range(1, heads):
        grad = grad + ua[source].astype(F32)
    dx_ref[...] = dh_ref[...] + centre_back(grad, xhat, scale)

    gain_tile[...] = jnp.zeros_like(gain_tile)
    gain_tile[0:1, 0:rows] = g1_ref[...].astype(F32)
    gain = jnp.transpose(jnp.broadcast_to(gain_tile[0:1, :], (LANES, LANES)))[:rows]
    low_half = lane_ids((rows, LANES)) < HALF
    finish(ghq_copies)
    finish(gh_copies)
    d_gain = jnp.zeros((rows, LANES), F32)
    for source in range(heads):
        both = [gh[source, :, i * LANES : (i + 1) * LANES].astype(F32) for i in range(2)]
        grads = (
            ghq[source].astype(F32) * HS ** (-0.5),
            jnp.where(low_half, both[0], both[1]),
            pltpu.roll(jnp.where(low_half, both[1], both[0]), HALF, 1),
        )
        for which, value in enumerate(grads):
            columns = slice(which * model + source * LANES, which * model + (source + 1) * LANES)
            d_gain = d_gain + value * w_ref[:, columns].astype(F32)
            dw_ref[:, columns] = value * gain
    finish(w3_copies)
    shared = w3[...].reshape(rows, w3.shape[-1]).astype(F32)
    shared_ref[:, 0:model] = shared[:, 0:model]
    gain_col = jnp.sum(d_gain, axis=1, keepdims=True)
    shared_ref[:, model : model + LANES] = jnp.where(
        lane_ids((rows, LANES)) == blks + 1, gain_col, shared[:, model : model + LANES]
    )
    finish(po_copies)
    parts = jnp.concatenate([pa_ref[...], pa[...]], axis=1).reshape(share_ref.shape[2], model)
    mixture = dot(share_ref[0], parts) + dot(share_ref[1], parts)
    y_ref[...] = (hidden_ref[...] + mixture).astype(BF16)

    for step, there, back, slot in directions:

        @pl.when(two_away(step))
        def _():
            for side in range(2):
                for half in range(2):
                    far_copy(step, slot, side, half).wait_send()

        @pl.when(there)
        def _():
            for side in range(2):
                for half in range(2):
                    near_copy(step, slot, side, half).wait_send()


def call_last(
    x, dh, dq, dkv, xa, wa, w_qkv, g1, grads, rx, win, wout, po, pa, hidden, share,
    bounds, q, kv, kvt, d_o, lse, delta, heads, blks,
):
    tokens, model = x.shape
    span = tokens * heads
    rows = w_qkv.shape[0]
    wide = model + LANES
    part = rows // heads
    ff = wout.shape[0]

    def block(*lead):
        return pltpu.VMEM((*lead, span, LANES), BF16)

    return pl.pallas_call(
        functools.partial(last_kernel, heads, blks),
        out_shape=(
            jax.ShapeDtypeStruct((tokens, model), BF16),
            jax.ShapeDtypeStruct((tokens, model), F32),
            jax.ShapeDtypeStruct((rows, 3 * model), F32),
            jax.ShapeDtypeStruct((rows, wide), F32),
            jax.ShapeDtypeStruct((model, ff), F32),
            jax.ShapeDtypeStruct((ff, model), F32),
        ),
        in_specs=hbm_specs(1) + vmem_specs(5) + hbm_specs(2) + vmem_specs(2) + hbm_specs(2) + vmem_specs(11),
        out_specs=tuple(vmem_specs(6)),
        scratch_shapes=[
            pltpu.VMEM((tokens, model), BF16),
            pltpu.VMEM((rows, 3 * model), BF16),
            pltpu.VMEM((1, rows), BF16),
            pltpu.VMEM(win.shape, BF16),
            pltpu.VMEM(wout.shape, BF16),
            dma(5),
            pltpu.VMEM((8, LANES), F32),
            block(4), block(4), block(2, 2), block(), pltpu.VMEM((span // 2, LANES), BF16),
            pltpu.VMEM((2, span, LANES), F32), pltpu.VMEM((span // 2, LANES), BF16),
            pltpu.VMEM((2, span, LANES), F32), block(),
            pltpu.VMEM((heads, tokens, model), BF16), pltpu.VMEM((heads, tokens, model), BF16),
            pltpu.VMEM((blks, rows, 2 * LANES), BF16), pltpu.VMEM((blks, rows, 2 * LANES), BF16),
            pltpu.VMEM((blks, rows, LANES), BF16), pltpu.VMEM((blks, rows, LANES), BF16),
            pltpu.VMEM((heads, tokens, model), F32), pltpu.VMEM((model, span), BF16),
            pltpu.VMEM(pa.shape, BF16),
            pltpu.VMEM((heads, rows, 2 * LANES), BF16), pltpu.VMEM((heads, rows, LANES), BF16),
            pltpu.VMEM((heads, blks, part, wide), BF16), pltpu.VMEM((blks, part, wide), BF16),
            pltpu.VMEM((blks, part, wide), BF16), pltpu.VMEM((heads, part, wide), BF16),
            pltpu.SemaphoreType.DMA, pltpu.SemaphoreType.DMA, pltpu.SemaphoreType.DMA, pltpu.SemaphoreType.DMA,
            dma(4, 2), dma(4, 2), dma(4, 2), dma(2, 2, 2),
            dma(heads), dma(heads), dma(blks), dma(blks), dma(heads), dma(heads), dma(heads), dma(heads),
            dma(blks), dma(blks), dma(heads), dma(heads), dma(2), dma(2), dma(blks), dma(blks), dma(blks), dma(blks), dma(heads), dma(heads),
            pltpu.VMEM((2, model, ff // 2), BF16), pltpu.VMEM((2, ff // 2, model), BF16),
        ],
        compiler_params=pltpu.CompilerParams(
            collective_id=3, has_side_effects=True, vmem_limit_bytes=36 * MIB
        ),
        name="last",
    )(
        *in_hbm(x), dh, dq, dkv, xa, wa, *in_hbm(w_qkv, g1.reshape(1, rows)),
        grads.reshape(blks, heads, part, wide), rx, *in_hbm(win, wout), po, pa, hidden, share,
        bounds, q, kv, kvt, d_o, lse, delta,
    )


def finish_kernel(
    experts,
    y_ref, dx_ref, dw_ref, shared_ref, din_ref, dout_ref,
    y_out, dx_out, g1_out, dw_out, dwo_out, g2_out, wr_out, din_out, dout_out,
    tile, wr, g2, g1, sem,
):
    rows = shared_ref.shape[0]
    model = dx_ref.shape[1]
    copies = [
        pltpu.make_async_copy(dx_ref, dx_out, sem.at[0]),
        pltpu.make_async_copy(dw_ref, dw_out, sem.at[1]),
        pltpu.make_async_copy(shared_ref.at[:, pl.ds(0, model)], dwo_out, sem.at[2]),
        pltpu.make_async_copy(y_ref, y_out, sem.at[6]),
        pltpu.make_async_copy(din_ref, din_out, sem.at[7]),
        pltpu.make_async_copy(dout_ref, dout_out, sem.at[8]),
    ]
    for copy in copies:
        copy.start()
    tile[...] = jnp.zeros_like(tile)
    tile[0:rows, :] = shared_ref[:, model : model + LANES]
    across = jnp.transpose(tile[...])[:, 0:rows]
    wr[...] = across[0:experts]
    g2[...] = across[experts : experts + 1]
    g1[...] = across[experts + 1 : experts + 2]
    for index, (src, dst) in enumerate(((wr, wr_out), (g2, g2_out), (g1, g1_out))):
        copies.append(pltpu.make_async_copy(src, dst, sem.at[3 + index]))
        copies[-1].start()
    for copy in copies:
        copy.wait()


def call_finish(output, dx, dw, shared, d_in, d_out):
    rows = shared.shape[0]
    model = dx.shape[1]
    experts = model // rows
    return pl.pallas_call(
        functools.partial(finish_kernel, experts),
        out_shape=(
            jax.ShapeDtypeStruct(output.shape, BF16),
            jax.ShapeDtypeStruct(dx.shape, F32),
            jax.ShapeDtypeStruct((1, rows), F32),
            jax.ShapeDtypeStruct(dw.shape, F32),
            jax.ShapeDtypeStruct((rows, model), F32),
            jax.ShapeDtypeStruct((1, rows), F32),
            jax.ShapeDtypeStruct((experts, rows), F32),
            jax.ShapeDtypeStruct(d_in.shape, F32),
            jax.ShapeDtypeStruct(d_out.shape, F32),
        ),
        in_specs=vmem_specs(6),
        out_specs=tuple(hbm_specs(9)),
        scratch_shapes=[
            pltpu.VMEM((LANES, LANES), F32),
            pltpu.VMEM((experts, rows), F32),
            pltpu.VMEM((1, rows), F32),
            pltpu.VMEM((1, rows), F32),
            dma(9),
        ],
        compiler_params=pltpu.CompilerParams(vmem_limit_bytes=16 * MIB),
        name="finish",
    )(output, dx, dw, shared, d_in, d_out)


def local_kernels(
    inputs, ln1_gain, w_qkv, w_out, ln2_gain, w_router,
    expert_in, expert_out, routes, priority, doc_lengths, d_out,
):
    heads, blks = lax.axis_size("head"), lax.axis_size("blk")
    model = inputs.shape[1]
    tokens = inputs.shape[0]
    win, wout = expert_in[0], expert_out[0]
    q, kv, xa, wa, wo, kvt, bounds, begun = call_qkv(
        inputs, w_qkv, ln1_gain, w_out, w_router, ln2_gain, doc_lengths, heads, blks
    )
    o, o_low, lse = call_forward(bounds, q, kv, kvt, begun)
    po, pa, hidden, share, dh, d_o, grads, rx = call_middle(
        inputs, o_low.reshape(2, heads, tokens // 2, LANES), wo.reshape(model, model + LANES),
        routes, priority, d_out, win, wout, heads, blks,
    )
    d_o = d_o.reshape(2 * heads * tokens // QUERY_TILE, -1, HALF, LANES)
    dq, dkv, delta = call_backward(bounds, q, kv, kvt, d_o, o, lse)
    ends = call_last(
        inputs, dh, dq, dkv, xa, wa, w_qkv, ln1_gain, grads, rx, win, wout,
        po, pa, hidden, share, bounds, q, kv, kvt, d_o, lse, delta, heads, blks,
    )
    output, d_inputs, d_gain_one, d_qkv, d_out_proj, d_gain_two, d_router, d_in, d_out_weight = call_finish(*ends)
    return (
        output,
        d_inputs,
        d_gain_one.reshape(-1),
        d_qkv,
        d_out_proj,
        d_gain_two.reshape(-1),
        d_router.T,
        d_in[None],
        d_out_weight[None],
    )


def solution(mesh):
    in_specs = (
        P(("blk", "head"), None),
        P("blk"),
        P("blk", None),
        P("blk", None),
        P("blk"),
        P("blk", None),
        P("blk", None, None),
        P("blk", None, None),
        P(("blk", "head"), None),
        P(("blk", "head"), None),
        P(),
        P(("blk", "head"), None),
    )
    out_specs = (
        P(("blk", "head"), None),
        P(("blk", "head"), None),
        P("blk"),
        P("blk", None),
        P("blk", None),
        P("blk"),
        P("blk", None),
        P("blk", None, None),
        P("blk", None, None),
    )
    fits = mesh.shape["head"] == 4 and mesh.shape["blk"] == 8
    body = local_kernels if fits else local
    return jax.shard_map(body, mesh=mesh, in_specs=in_specs, out_specs=out_specs, check_vma=False)
```

profile of v0, /device:TPU:0, one launch (start us, length us, event | category | flops | bytes accessed | tf_op | source)
XLA Modules:
  0.0 117.1 jit_solution(6753631550047319417)
XLA Ops:
  0.6 28.3 %qkv.1 = (bf16[2,512,128]{2,1,0:T(8,128)(2,1)S(1)}, bf16[8,512,128]{2,1,0:T(8,128)(2,1)S(1)}, bf16[4,128,512]{2,1,0:T(8,128)(2,1)S(1)}, bf16[8,64,384]{2,1,0:T(8...) custom-call(bf16[128,512]{1,0:T(8,128)(2,1)} %x_hbm.5, ...), custom_call_target="tpu_custom_call" | custom-call | tf_op jit(solution)/shard_map/qkv/pallas_call | solution.py:804
  29.0 5.4 %attend.1 = (f32[4,256,128]{2,1,0:T(8,128)S(1)}, bf16[4,2,64,128]{3,2,1,0:T(8,128)(2,1)S(1)}, f32[4,8,256]{2,1,0:T(8,128)S(1)}) custom-call(s32[8,1024]{1,0:T(8,128)S(1)} %get-tuple-element.46.bounds_ref, bf16[2,512,128]{2,1,0:T(8,128)(2,1)S(1)} %get-tuple-element.47.q_ref, bf16[8,512,128]{2,1,0:T(8,128)(2,1)S(1)} %get-tuple-element.48.kv_ref, ...), custom_call_target="tpu_custom_call" | custom-call | tf_op jit(solution)/shard_map/attend/pallas_call | solution.py:881
  34.4 36.3 %experts.1 = (bf16[8,32,512]{2,1,0:T(8,128)(2,1)S(1)}, bf16[8,16,512]{2,1,0:T(8,128)(2,1)S(1)}, f32[128,512]{1,0:T(8,128)S(1)}, bf16[2,128,256]{2,1,0:T(8,128)(2...) custom-call(bf16[128,512]{1,0:T(8,128)(2,1)} %x_hbm.5, ...), custom_call_target="tpu_custom_call" | custom-call | tf_op jit(solution)/shard_map/experts/pallas_call | solution.py:1254
  70.7 6.9 %attend_back.1 = (f32[4,128,256]{2,1,0:T(8,128)S(1)}, bf16[8,512,128]{2,1,0:T(8,128)(2,1)S(1)}, f32[4,8,256]{2,1,0:T(8,128)S(1)}) custom-call(s32[8,1024]{1,0:T(8,128)S(1)} %get-tuple-element.46.bounds_ref, bf16[2,512,128]{2,1,0:T(8,128)(2,1)S(1)} %get-tuple-element.47.q_ref, bf16[8,512,128]{2,1,0:T(8,128)(2,1)S(1)} %get-tuple-element.48.kv_ref, ...), custom_call_target="tpu_custom_call" | custom-call | tf_op jit(solution)/shard_map/attend_back/pallas_call | solution.py:930
  77.6 35.5 %last.1 = (bf16[128,512]{1,0:T(8,128)(2,1)S(1)}, f32[128,512]{1,0:T(8,128)S(1)}, f32[64,1536]{1,0:T(8,128)S(1)}, f32[64,640]{1,0:T(8,128)S(1)}, f32[512,2048]{1,0:T(8,128)S(1)}, /*index=5*/f32[2048,512]{1,0:T(8,128)S(1)}) custom-call(bf16[128,512]{1,0:T(8,128)(2,1)} %x_hbm.5, f32[128,512]{1,0:T(8,128)S(1)} %get-tuple-element.53.dh_ref, ...), custom_call_target="tpu_custom_call" | custom-call | tf_op jit(solution)/shard_map/last/pallas_call | solution.py:1668
  113.2 3.8 %finish.1 = (bf16[128,512]{1,0:T(8,128)(2,1)}, f32[128,512]{1,0:T(8,128)}, f32[1,64]{1,0:T(1,128)}, f32[64,1536]{1,0:T(8,128)}, f32[64,512]{1,0:T(8,128)}, /*ind...) custom-call(bf16[128,512]{1,0:T(8,128)(2,1)S(1)} %get-tuple-element.68.y_ref, ...), custom_call_target="tpu_custom_call" | custom-call | tf_op jit(solution)/shard_map/finish/pallas_call | solution.py:1751
where the time goes:
time: 117 us
  Pallas kernels  116 us (99%)
    pallas_call x1, Pallas kernels, call_middle(): pl.pallas_call(functools.partial(middle_kernel, heads, blks), out_shape=(...  36.3 us
    pallas_call x1, Pallas kernels, call_last(): pl.pallas_call(functools.partial(last_kernel, heads, blks), out_shape=(ja...  35.5 us
    pallas_call x1, Pallas kernels, call_qkv(): pl.pallas_call(functools.partial(qkv_kernel, heads, blks), out_shape=(jax...  28.3 us
    pallas_call x1, Pallas kernels, call_backward(): pl.pallas_call(backward_kernel, out_shape=(jax.ShapeDtypeStruct((tiles, L...  6.92 us
    pallas_call x1, Pallas kernels, call_forward(): pl.pallas_call(forward_kernel, out_shape=(jax.ShapeDtypeStruct((tiles, QU...  5.37 us
    pallas_call x1, Pallas kernels, call_finish(): pl.pallas_call(functools.partial(finish_kernel, experts), out_shape=(jax....  3.78 us

commit v1 on v0

--- a/solution.py
+++ b/solution.py
@@ -981,7 +981,7 @@
     x_hbm, o_ref, wo_ref, routes_hbm, rank_hbm, d_out_hbm, win_hbm, wout_hbm,
     po, pa, hidden_ref, share_ref, dh_ref, dma_all, grads_ref, rx,
     x_ref, routes_ref, rank_ref, d_out_ref, win_ref, wout_ref, rows_in, in_sem,
-    o_all, dos, doa, rs, ra, dr, da, dms, acc_out, acc_row, mix, gate_rows, d_gate_rows, turned,
+    o_all, dos, doa, rs, ra, dr, da, dms, mix, gate_rows, d_gate_rows, turned,
     o_send, o_recv, dos_send, dos_recv, r_send, r_recv,
     dr_send, dr_recv, dm_send, dm_recv, rx_send, rx_recv, g_send, g_recv, dg_send, dg_recv, pa_send, pa_recv,
 ):
@@ -1115,8 +1115,6 @@
         for k in range(1, blks)
     ]
     start(g_copies)
-    acc_out[...] = jnp.zeros_like(acc_out)
-    acc_row[...] = jnp.zeros_like(acc_row)
     finish(dos_copies)
     finish(r_copies)
 
@@ -1148,25 +1146,16 @@
     ]
     start(to_across)
     to_sibling.start()
-    half_ff = wout_ref.shape[0] // 4
     for copy in fetched[4:]:
         copy.wait()
-
-    @pl.loop(0, 4)
-    def _(chunk):
-        first = pl.multiple_of(chunk * half_ff, half_ff)
-        into = win_ref[:, pl.ds(first, half_ff)]
-        outof = wout_ref[pl.ds(first, half_ff), :]
-        act, slope = gelu_parts(dot(rx[head, :, 0:model], into))
-        acc_out[...] += dot(act.astype(BF16), outof)
-        d_act = dot(rx[head, :, model : 2 * model], outof, (1, 1))
-        acc_row[...] += dot((slope * d_act).astype(BF16), into, (1, 1))
-
-    result = acc_out[...].astype(BF16)
-    d_gate = jnp.sum(out_rows.astype(F32) * result.astype(F32), axis=1, keepdims=True)
-    dr[...] = acc_row[...].astype(BF16).reshape(dr.shape)
+    act, slope = gelu_parts(dot(rx[head, :, 0:model], win_ref[...]))
+    d_act = dot(rx[head, :, model : 2 * model], wout_ref[...], (1, 1))
+    row_grads = dot((slope * d_act).astype(BF16), win_ref[...], (1, 1))
+    dr[...] = row_grads.astype(BF16).reshape(dr.shape)
     dr_copies = blk_copies(dr, da, dr_send, dr_recv)
     start(dr_copies)
+    result = dot(act.astype(BF16), wout_ref[...]).astype(BF16)
+    d_gate = jnp.sum(out_rows.astype(F32) * result.astype(F32), axis=1, keepdims=True)
     da[blk] = dr[blk]
     d_wide = jnp.broadcast_to(d_gate, (slots, LANES))
     d_gate_rows[blk] = jnp.concatenate(
@@ -1276,7 +1265,6 @@
             dma(6),
             block(2, heads), rows(model), rows(model), rows(model), rows(model),
             rows(model), rows(model), block(2, heads),
-            pltpu.VMEM((slots, model), F32), pltpu.VMEM((slots, model), F32),
             pltpu.VMEM((tokens, model), BF16),
             pltpu.VMEM((blks, 1, slots), F32), pltpu.VMEM((blks, 1, slots), F32),
             pltpu.VMEM((slots, LANES), F32),
@@ -1455,10 +1443,22 @@
     even = y == 0
 
 
+    def wide_copies(part):
+        some = pl.ds(part * ff_half // 2, ff_half // 2)
+        ins = din_half.at[core, :, some]
+        outs = dout_half.at[core, some]
+        return [
+            remote(ins, ins, e_send.at[part, 0], e_recv.at[part, 0], sibling, blk),
+            remote(outs, outs, e_send.at[part, 1], e_recv.at[part, 1], sibling, blk),
+        ]
+
+    e_copies = [wide_copies(part) for part in range(2)]
+
     @pl.loop(0, 2)
     def _(chunk):
         expert_chunk(chunk)
 
+    start(e_copies[0])
     q_copy.wait()
     landed = dq_all[...].astype(F32)
     landed = jnp.concatenate([landed, pltpu.roll(landed, HALF, 1)], axis=0)
@@ -1495,11 +1495,7 @@
     def _(chunk):
         expert_chunk(chunk)
 
-    e_copies = [
-        remote(din_half.at[core], din_half.at[core], e_send.at[0], e_recv.at[0], sibling, blk),
-        remote(dout_half.at[core], dout_half.at[core], e_send.at[1], e_recv.at[1], sibling, blk),
-    ]
-    start(e_copies)
+    start(e_copies[1])
 
     pair_copy.wait()
     for step, there, back, slot in directions:
@@ -1576,10 +1572,13 @@
     start(w3_copies)
 
     xhat, scale = centre(x_ref[...].astype(F32))
-    finish(e_copies)
-    there = pl.multiple_of((1 - core) * ff_half, ff_half)
-    din_ref[:, pl.ds(there, ff_half)] = din_half[1 - core].astype(F32)
-    dout_ref[pl.ds(there, ff_half), :] = dout_half[1 - core].astype(F32)
+    for part in range(2):
+        finish(e_copies[part])
+        size = ff_half // 2
+        there = pl.multiple_of((1 - core) * ff_half + part * size, size)
+        here = slice(part * size, (part + 1) * size)
+        din_ref[:, pl.ds(there, size)] = din_half[1 - core, :, here].astype(F32)
+        dout_ref[pl.ds(there, size), :] = dout_half[1 - core, here].astype(F32)
     finish(g_copies)
     total = ga[0].astype(F32)
     for source in range(1, blks):
@@ -1699,7 +1698,7 @@
             pltpu.SemaphoreType.DMA, pltpu.SemaphoreType.DMA, pltpu.SemaphoreType.DMA, pltpu.SemaphoreType.DMA,
             dma(4, 2), dma(4, 2), dma(4, 2), dma(2, 2, 2),
             dma(heads), dma(heads), dma(blks), dma(blks), dma(heads), dma(heads), dma(heads), dma(heads),
-            dma(blks), dma(blks), dma(heads), dma(heads), dma(2), dma(2), dma(blks), dma(blks), dma(blks), dma(blks), dma(heads), dma(heads),
+            dma(blks), dma(blks), dma(heads), dma(heads), dma(2, 2), dma(2, 2), dma(blks), dma(blks), dma(blks), dma(blks), dma(heads), dma(heads),
             pltpu.VMEM((2, model, ff // 2), BF16), pltpu.VMEM((2, ff // 2, model), BF16),
         ],
         compiler_params=pltpu.CompilerParams(

time: 117 us -> 118 us (level)
    pallas_call x1, Pallas kernels: 35.5 us -> 42.3 us  [call_last(): pl.pallas_call(functools.partial(last_kernel, heads, blks), out_shape=(ja...]
    pallas_call x1, Pallas kernels: 6.92 us -> 2.08 us  [call_backward(): pl.pallas_call(backward_kernel, out_shape=(jax.ShapeDtypeStruct((tiles, L...]
    pallas_call x1, Pallas kernels: 5.37 us -> 1.78 us  [call_forward(): pl.pallas_call(forward_kernel, out_shape=(jax.ShapeDtypeStruct((tiles, QU...]
    pallas_call x1, Pallas kernels: 36.3 us -> 39.1 us  [call_middle(): pl.pallas_call(functools.partial(middle_kernel, heads, blks), out_shape=(...]
where the time goes in v1:
time: 118 us
  Pallas kernels  117 us (99%)
    pallas_call x1, Pallas kernels, call_last(): pl.pallas_call(functools.partial(last_kernel, heads, blks), out_shape=(ja...  42.3 us
    pallas_call x1, Pallas kernels, call_middle(): pl.pallas_call(functools.partial(middle_kernel, heads, blks), out_shape=(...  39.1 us
    pallas_call x1, Pallas kernels, call_qkv(): pl.pallas_call(functools.partial(qkv_kernel, heads, blks), out_shape=(jax...  28.3 us
    pallas_call x1, Pallas kernels, call_finish(): pl.pallas_call(functools.partial(finish_kernel, experts), out_shape=(jax....  3.78 us

profile of v1, /device:TPU:0, one launch (start us, length us, event | category | flops | bytes accessed | tf_op | source)
XLA Modules:
  0.0 118.3 jit_solution(3577191284672852845)
XLA Ops:
  0.6 28.3 %qkv.1 = (bf16[2,512,128]{2,1,0:T(8,128)(2,1)S(1)}, bf16[8,512,128]{2,1,0:T(8,128)(2,1)S(1)}, bf16[4,128,512]{2,1,0:T(8,128)(2,1)S(1)}, bf16[8,64,384]{2,1,0:T(8...) custom-call(bf16[128,512]{1,0:T(8,128)(2,1)} %x_hbm.5, ...), custom_call_target="tpu_custom_call" | custom-call | tf_op jit(solution)/shard_map/qkv/pallas_call | solution.py:804
  29.0 1.8 %attend.1 = (f32[4,256,128]{2,1,0:T(8,128)S(1)}, bf16[4,2,64,128]{3,2,1,0:T(8,128)(2,1)S(1)}, f32[4,8,256]{2,1,0:T(8,128)S(1)}) custom-call(s32[8,1024]{1,0:T(8,128)S(1)} %get-tuple-element.46.bounds_ref, bf16[2,512,128]{2,1,0:T(8,128)(2,1)S(1)} %get-tuple-element.47.q_ref, bf16[8,512,128]{2,1,0:T(8,128)(2,1)S(1)} %get-tuple-element.48.kv_ref, ...), custom_call_target="tpu_custom_call" | custom-call | tf_op jit(solution)/shard_map/attend/pallas_call | solution.py:881
  30.8 39.1 %experts.1 = (bf16[8,32,512]{2,1,0:T(8,128)(2,1)S(1)}, bf16[8,16,512]{2,1,0:T(8,128)(2,1)S(1)}, f32[128,512]{1,0:T(8,128)S(1)}, bf16[2,128,256]{2,1,0:T(8,128)(2...) custom-call(bf16[128,512]{1,0:T(8,128)(2,1)} %x_hbm.5, ...), custom_call_target="tpu_custom_call" | custom-call | tf_op jit(solution)/shard_map/experts/pallas_call | solution.py:1243
  69.9 2.1 %attend_back.1 = (f32[4,128,256]{2,1,0:T(8,128)S(1)}, bf16[8,512,128]{2,1,0:T(8,128)(2,1)S(1)}, f32[4,8,256]{2,1,0:T(8,128)S(1)}) custom-call(s32[8,1024]{1,0:T(8,128)S(1)} %get-tuple-element.46.bounds_ref, bf16[2,512,128]{2,1,0:T(8,128)(2,1)S(1)} %get-tuple-element.47.q_ref, bf16[8,512,128]{2,1,0:T(8,128)(2,1)S(1)} %get-tuple-element.48.kv_ref, ...), custom_call_target="tpu_custom_call" | custom-call | tf_op jit(solution)/shard_map/attend_back/pallas_call | solution.py:930
  72.0 42.3 %last.1 = (bf16[128,512]{1,0:T(8,128)(2,1)S(1)}, f32[128,512]{1,0:T(8,128)S(1)}, f32[64,1536]{1,0:T(8,128)S(1)}, f32[64,640]{1,0:T(8,128)S(1)}, f32[512,2048]{1,0:T(8,128)S(1)}, /*index=5*/f32[2048,512]{1,0:T(8,128)S(1)}) custom-call(bf16[128,512]{1,0:T(8,128)(2,1)} %x_hbm.5, f32[128,512]{1,0:T(8,128)S(1)} %get-tuple-element.53.dh_ref, ...), custom_call_target="tpu_custom_call" | custom-call | tf_op jit(solution)/shard_map/last/pallas_call | solution.py:1667
  114.3 3.8 %finish.1 = (bf16[128,512]{1,0:T(8,128)(2,1)}, f32[128,512]{1,0:T(8,128)}, f32[1,64]{1,0:T(1,128)}, f32[64,1536]{1,0:T(8,128)}, f32[64,512]{1,0:T(8,128)}, /*ind...) custom-call(bf16[128,512]{1,0:T(8,128)(2,1)S(1)} %get-tuple-element.68.y_ref, ...), custom_call_target="tpu_custom_call" | custom-call | tf_op jit(solution)/shard_map/finish/pallas_call | solution.py:1750

commit v2 on v1

--- a/solution.py
+++ b/solution.py
@@ -1365,7 +1365,7 @@
     core = lax.rem(head, 2)
     sibling = head - core + 1 - core
     ff_half = wout_ref.shape[0] // 2
-    ff_step = ff_half // 4
+    ff_step = ff_half // 2
 
     def expert_chunk(chunk):
         here = pl.multiple_of(core * ff_half + chunk * ff_step, ff_step)
@@ -1454,9 +1454,7 @@
 
     e_copies = [wide_copies(part) for part in range(2)]
 
-    @pl.loop(0, 2)
-    def _(chunk):
-        expert_chunk(chunk)
+    expert_chunk(0)
 
     start(e_copies[0])
     q_copy.wait()
@@ -1491,9 +1489,7 @@
     start(w2_copies)
     w2[blk] = w2s[blk]
 
-    @pl.loop(2, 4)
-    def _(chunk):
-        expert_chunk(chunk)
+    expert_chunk(1)
 
     start(e_copies[1])
 

time: 118 us -> 118 us (level)
  no operation moved by 1% of the time
where the time goes in v2:
time: 118 us
  Pallas kernels  117 us (99%)
    pallas_call x1, Pallas kernels, call_last(): pl.pallas_call(functools.partial(last_kernel, heads, blks), out_shape=(ja...  42.4 us
    pallas_call x1, Pallas kernels, call_middle(): pl.pallas_call(functools.partial(middle_kernel, heads, blks), out_shape=(...  38.6 us
    pallas_call x1, Pallas kernels, call_qkv(): pl.pallas_call(functools.partial(qkv_kernel, heads, blks), out_shape=(jax...  28.3 us
    pallas_call x1, Pallas kernels, call_finish(): pl.pallas_call(functools.partial(finish_kernel, experts), out_shape=(jax....  3.78 us

profile of v2, /device:TPU:0, one launch (start us, length us, event | category | flops | bytes accessed | tf_op | source)
XLA Modules:
  0.0 117.9 jit_solution(5097263139061789316)
XLA Ops:
  0.6 28.3 %qkv.1 = (bf16[2,512,128]{2,1,0:T(8,128)(2,1)S(1)}, bf16[8,512,128]{2,1,0:T(8,128)(2,1)S(1)}, bf16[4,128,512]{2,1,0:T(8,128)(2,1)S(1)}, bf16[8,64,384]{2,1,0:T(8...) custom-call(bf16[128,512]{1,0:T(8,128)(2,1)} %x_hbm.5, ...), custom_call_target="tpu_custom_call" | custom-call | tf_op jit(solution)/shard_map/qkv/pallas_call | solution.py:804
  29.0 1.8 %attend.1 = (f32[4,256,128]{2,1,0:T(8,128)S(1)}, bf16[4,2,64,128]{3,2,1,0:T(8,128)(2,1)S(1)}, f32[4,8,256]{2,1,0:T(8,128)S(1)}) custom-call(s32[8,1024]{1,0:T(8,128)S(1)} %get-tuple-element.46.bounds_ref, bf16[2,512,128]{2,1,0:T(8,128)(2,1)S(1)} %get-tuple-element.47.q_ref, bf16[8,512,128]{2,1,0:T(8,128)(2,1)S(1)} %get-tuple-element.48.kv_ref, ...), custom_call_target="tpu_custom_call" | custom-call | tf_op jit(solution)/shard_map/attend/pallas_call | solution.py:881
  30.8 38.6 %experts.1 = (bf16[8,32,512]{2,1,0:T(8,128)(2,1)S(1)}, bf16[8,16,512]{2,1,0:T(8,128)(2,1)S(1)}, f32[128,512]{1,0:T(8,128)S(1)}, bf16[2,128,256]{2,1,0:T(8,128)(2...) custom-call(bf16[128,512]{1,0:T(8,128)(2,1)} %x_hbm.5, ...), custom_call_target="tpu_custom_call" | custom-call | tf_op jit(solution)/shard_map/experts/pallas_call | solution.py:1243
  69.4 2.1 %attend_back.1 = (f32[4,128,256]{2,1,0:T(8,128)S(1)}, bf16[8,512,128]{2,1,0:T(8,128)(2,1)S(1)}, f32[4,8,256]{2,1,0:T(8,128)S(1)}) custom-call(s32[8,1024]{1,0:T(8,128)S(1)} %get-tuple-element.46.bounds_ref, bf16[2,512,128]{2,1,0:T(8,128)(2,1)S(1)} %get-tuple-element.47.q_ref, bf16[8,512,128]{2,1,0:T(8,128)(2,1)S(1)} %get-tuple-element.48.kv_ref, ...), custom_call_target="tpu_custom_call" | custom-call | tf_op jit(solution)/shard_map/attend_back/pallas_call | solution.py:930
  71.5 42.4 %last.1 = (bf16[128,512]{1,0:T(8,128)(2,1)S(1)}, f32[128,512]{1,0:T(8,128)S(1)}, f32[64,1536]{1,0:T(8,128)S(1)}, f32[64,640]{1,0:T(8,128)S(1)}, f32[512,2048]{1,0:T(8,128)S(1)}, /*index=5*/f32[2048,512]{1,0:T(8,128)S(1)}) custom-call(bf16[128,512]{1,0:T(8,128)(2,1)} %x_hbm.5, f32[128,512]{1,0:T(8,128)S(1)} %get-tuple-element.53.dh_ref, ...), custom_call_target="tpu_custom_call" | custom-call | tf_op jit(solution)/shard_map/last/pallas_call | solution.py:1663
  113.9 3.8 %finish.1 = (bf16[128,512]{1,0:T(8,128)(2,1)}, f32[128,512]{1,0:T(8,128)}, f32[1,64]{1,0:T(1,128)}, f32[64,1536]{1,0:T(8,128)}, f32[64,512]{1,0:T(8,128)}, /*ind...) custom-call(bf16[128,512]{1,0:T(8,128)(2,1)S(1)} %get-tuple-element.68.y_ref, ...), custom_call_target="tpu_custom_call" | custom-call | tf_op jit(solution)/shard_map/finish/pallas_call | solution.py:1746
